TPU v7x, 32 devices: a whole 2x2x4 slice. The times are simulated.
32 devices in a mesh: shot: 4 (over y, core), gx: 4 (over z), gy: 2 (over x).
Axes of the slice: x: 2, y: 2, z: 4, core: 2. Of those that a mesh axis runs over, the one named last changes fastest.
Arguments:
- latent: float32 [32, 24, 1024], P('shot', 'gx', 'gy'), may hold values from -6 to 6
- w_first: float32 [64, 64], replicated, may hold values from -0.75 to 0.75
- w_second: float32 [64, 128], replicated, may hold values from -0.75 to 0.75
- fwd_press: float32 [4, 96, 64, 128], P('shot', 'gx', 'gy'), may hold values from -1.5 to 8
- fwd_vel: float32 [4, 3, 96, 64, 128], P('shot', None, 'gx', 'gy'), may hold values from -1.5 to 8
- adj_press: float32 [4, 96, 64, 128], P('shot', 'gx', 'gy'), may hold values from -1.5 to 8
- adj_vel: float32 [4, 3, 96, 64, 128], P('shot', None, 'gx', 'gy'), may hold values from -1.5 to 8
- src_pos: int32 [3, 4], P(None, 'shot'), may hold values from 0 to 127, as said below
- src_amp: float32 [3, 4], P(None, 'shot'), may hold values from -24 to 24
- rec_pos: int32 [4, 3, 2048], P('shot'), may hold values from 0 to 127, as said below
- observed: float32 [4, 3, 2048], P('shot'), may hold values from -6 to 6
Outputs:
- grad_latent: float32 [32, 24, 1024], P('shot', 'gx', 'gy')
- grad_first: float32 [64, 64], replicated
- grad_second: float32 [64, 128], replicated
Inputs may be any that keep to these rules, and one draw needn't show every extreme that they name: `src_pos`: row 0 is an x cell below 96, row 1 a y cell below 64, row 2 a depth cell below 128. `rec_pos`: component 0 is an x cell below 96, component 1 a y cell below 64, component 2 a depth cell below 128; cells may repeat.
All inputs are finite; a program needn't handle non-finite values.
Results may differ from a plain program's by a relative error of at most 0.0003.
Values sent between devices are 32-bit elements; how exact they have to be, the bound alone decides.
A program may use at most 64 MiB of HBM per device.

v0:
```python
import jax
import jax.numpy as jnp
from jax import lax
from jax.sharding import PartitionSpec as P

CH = 64
STEPS = 3
coeffs = (1225.0 / 1024.0, -245.0 / 3072.0, 49.0 / 5120.0, -5.0 / 7168.0)


def with_halo(block, sides, width):
    for axis, dim in sides:
        count = lax.axis_size(axis)
        forward = [(i, i + 1) for i in range(count - 1)]
        backward = [(target, source) for source, target in forward]
        low = lax.ppermute(
            lax.slice_in_dim(block, block.shape[dim] - width, None, axis=dim), axis, forward
        )
        high = lax.ppermute(lax.slice_in_dim(block, 0, width, axis=dim), axis, backward)
        block = jnp.concatenate([low, block, high], axis=dim)
    return block


def take_slab(values_in, axis_id, start_at, length):
    return lax.slice_in_dim(values_in, start_at, start_at + length, axis=axis_id)


def diff_plus(extended, axis_id, start_at, length):
    summed = 0.0
    for order, weight in enumerate(coeffs):
        offset = order + 1
        summed = summed + weight * (
            take_slab(extended, axis_id, start_at + offset, length)
            - take_slab(extended, axis_id, start_at - offset + 1, length)
        )
    return summed


def diff_minus(extended, axis_id, start_at, length):
    summed = 0.0
    for order, weight in enumerate(coeffs):
        offset = order + 1
        summed = summed + weight * (
            take_slab(extended, axis_id, start_at + offset - 1, length)
            - take_slab(extended, axis_id, start_at - offset, length)
        )
    return summed


def depth_pad(field_in):
    return jnp.pad(field_in, ((0, 0), (0, 0), (4, 4)))


def rim_x(field_in):
    return with_halo(field_in, (("gx", 0),), 4)


def rim_y(field_in):
    return with_halo(field_in, (("gy", 1),), 4)


def wide_step(fields, modulus, buoy_x, buoy_y, buoyancy):
    pressure, ext_x, ext_y, vel_z = fields
    size_x, size_y, size_z = pressure.shape
    slope_x = diff_plus(with_halo(pressure, (("gx", 0),), 8), 0, 4, size_x + 8)
    slope_y = diff_plus(with_halo(pressure, (("gy", 1),), 8), 1, 4, size_y + 8)
    grad_z = diff_plus(depth_pad(pressure), 2, 4, size_z)
    ext_x = ext_x - buoy_x * slope_x
    ext_y = ext_y - buoy_y * slope_y
    vel_z = vel_z - buoyancy * grad_z
    diverge = (
        diff_minus(ext_x, 0, 4, size_x)
        + diff_minus(ext_y, 1, 4, size_y)
        + diff_minus(depth_pad(vel_z), 2, 4, size_z)
    )
    pressure = pressure - modulus * diverge
    slopes = (slope_x[4 : 4 + size_x], slope_y[:, 4 : 4 + size_y], grad_z)
    own_vel = (ext_x[4 : 4 + size_x], ext_y[:, 4 : 4 + size_y], vel_z)
    return ((pressure, ext_x, ext_y, vel_z), diverge, slopes, own_vel)


def decode(latent, w_first, w_second):
    depth_c, rows_x, merged = latent.shape
    rows_y = merged // CH
    flattened = latent.reshape(-1, CH)
    hidden = jnp.tanh(jnp.dot(flattened, w_first, precision=lax.Precision.HIGHEST))
    outputs = jnp.dot(hidden, w_second, precision=lax.Precision.HIGHEST)
    fine_out = (
        outputs.reshape(depth_c, rows_x, rows_y, 2, 4, 4, 4)
        .transpose(3, 1, 4, 2, 5, 0, 6)
        .reshape(2, rows_x * 4, rows_y * 4, depth_c * 4)
    )
    return (flattened, hidden, fine_out)


def materials(fine_out):
    wave_speed = 0.15 + 0.25 * jax.nn.sigmoid(fine_out[0])
    density = 1.0 + 1.5 * jax.nn.sigmoid(fine_out[1])
    return (density * wave_speed * wave_speed, 1.0 / density)


def decoder_grads(flattened, hidden, fine_out, grad_mod, grad_buoy, w_first, w_second):
    sig_speed = jax.nn.sigmoid(fine_out[0])
    sig_dens = jax.nn.sigmoid(fine_out[1])
    wave_speed = 0.15 + 0.25 * sig_speed
    density = 1.0 + 1.5 * sig_dens
    grad_speed = grad_mod * 2.0 * density * wave_speed
    grad_dens = grad_mod * wave_speed * wave_speed - grad_buoy / (density * density)
    grad_fine = jnp.stack(
        [
            grad_speed * 0.25 * sig_speed * (1.0 - sig_speed),
            grad_dens * 1.5 * sig_dens * (1.0 - sig_dens),
        ]
    )
    size_x, size_y, size_z = (grad_fine.shape[1], grad_fine.shape[2], grad_fine.shape[3])
    grad_out = (
        grad_fine.reshape(2, size_x // 4, 4, size_y // 4, 4, size_z // 4, 4)
        .transpose(5, 1, 3, 0, 2, 4, 6)
        .reshape(-1, 128)
    )
    grad_hidden = jnp.dot(grad_out, w_second.T, precision=lax.Precision.HIGHEST)
    grad_pre = grad_hidden * (1.0 - hidden * hidden)
    grad_latent = jnp.dot(grad_pre, w_first.T, precision=lax.Precision.HIGHEST).reshape(
        size_z // 4, size_x // 4, size_y // 4 * CH
    )
    grad_second = jnp.dot(hidden.T, grad_out, precision=lax.Precision.HIGHEST)
    grad_first = jnp.dot(flattened.T, grad_pre, precision=lax.Precision.HIGHEST)
    return (grad_latent, grad_first, grad_second)


def receiver_fields(receivers, observed_now, anchor_x, anchor_y, size_x, size_y, size_z):
    local_x = receivers[0] - anchor_x
    local_y = receivers[1] - anchor_y
    inside = (local_x >= 0) & (local_x < size_x) & (local_y >= 0) & (local_y < size_y)
    column = jnp.where(inside, local_x * size_y + local_y, -1)
    count = column.shape[0]
    picks = (
        lax.broadcasted_iota(jnp.int32, (size_x * size_y, count), 0) == column[None, :]
    ).astype(jnp.bfloat16)
    depth = (lax.broadcasted_iota(jnp.int32, (count, size_z), 1) == receivers[2][:, None]).astype(
        jnp.float32
    )
    high = lax.reduce_precision(observed_now, 8, 7)
    low = lax.reduce_precision(observed_now - high, 8, 7)
    parts = [depth]
    for moment in range(STEPS):
        parts = parts + [depth * high[moment][:, None], depth * low[moment][:, None]]
    weights = jnp.concatenate(parts, axis=1).astype(jnp.bfloat16)
    summed = jnp.dot(picks, weights, preferred_element_type=jnp.float32)
    planes = summed.reshape(size_x, size_y, len(parts), size_z)
    recorded = [planes[:, :, 1 + 2 * m] + planes[:, :, 2 + 2 * m] for m in range(STEPS)]
    return (planes[:, :, 0], recorded)


def body(
    latent,
    w_first,
    w_second,
    fwd_press,
    fwd_vel,
    adj_press,
    adj_vel,
    src_pos,
    src_amp,
    rec_pos,
    observed,
):
    size_x, size_y = (fwd_press.shape[1], fwd_press.shape[2])
    anchor_x = lax.axis_index("gx") * size_x
    anchor_y = lax.axis_index("gy") * size_y
    flattened, hidden, fine_out = decode(latent, w_first, w_second)
    slab_mod, slab_buoy = materials(fine_out)
    stacked = lax.all_gather(jnp.stack([slab_mod, slab_buoy]), "shot", axis=3, tiled=True)
    modulus, buoyancy = (stacked[0], stacked[1])
    buoy_x = rim_x(buoyancy)
    buoy_y = rim_y(buoyancy)

    def prepare(vel_x, vel_y):
        return (rim_x(vel_x), rim_y(vel_y))

    def advance(fields):
        return wide_step(fields, modulus, buoy_x, buoy_y, buoyancy)

    def one_shot(totals, inputs):
        grad_mod, grad_buoy = totals
        (
            start_press,
            start_vel,
            back_press,
            back_vel,
            source,
            amplitudes,
            receivers,
            observed_now,
        ) = inputs
        size_z = start_press.shape[2]
        at_source = (
            (lax.broadcasted_iota(jnp.int32, start_press.shape, 0) == source[0] - anchor_x)
            & (lax.broadcasted_iota(jnp.int32, start_press.shape, 1) == source[1] - anchor_y)
            & (lax.broadcasted_iota(jnp.int32, start_press.shape, 2) == source[2])
        )
        hits, recorded = receiver_fields(
            receivers, observed_now, anchor_x, anchor_y, size_x, size_y, size_z
        )
        fields = (start_press,) + prepare(start_vel[0], start_vel[1]) + (start_vel[2],)
        stored = []
        misfits = []
        for moment in range(STEPS):
            fields, diverge, slopes, own_vel = advance(fields)
            pressure = fields[0] + jnp.where(at_source, amplitudes[moment], 0.0)
            fields = (pressure,) + fields[1:]
            misfits.append(hits * pressure - recorded[moment])
            stored.append((diverge, slopes))
        fields = (back_press,) + prepare(back_vel[0], back_vel[1]) + (back_vel[2],)
        for moment in reversed(range(STEPS)):
            pressure = fields[0] + misfits[moment]
            fields, diverge, slopes, own_vel = advance((pressure,) + fields[1:])
            grad_mod = grad_mod - fields[0] * stored[moment][0]
            grad_buoy = grad_buoy - (
                own_vel[0] * stored[moment][1][0]
                + own_vel[1] * stored[moment][1][1]
                + own_vel[2] * stored[moment][1][2]
            )
        return ((grad_mod, grad_buoy), None)

    zeros = jnp.zeros(modulus.shape, jnp.float32)
    totals, _ignored = lax.scan(
        one_shot,
        (zeros, zeros),
        (fwd_press, fwd_vel, adj_press, adj_vel, src_pos.T, src_amp.T, rec_pos, observed),
    )
    shares = lax.psum_scatter(
        jnp.stack([totals[0], totals[1]]), "shot", scatter_dimension=3, tiled=True
    )
    grad_latent, grad_first, grad_second = decoder_grads(
        flattened, hidden, fine_out, shares[0], shares[1], w_first, w_second
    )
    grad_first, grad_second = lax.psum((grad_first, grad_second), ("shot", "gx", "gy"))
    return (grad_latent, grad_first, grad_second)


def solution(mesh):
    in_specs = (
        P("shot", "gx", "gy"),
        P(),
        P(),
        P("shot", "gx", "gy", None),
        P("shot", None, "gx", "gy", None),
        P("shot", "gx", "gy", None),
        P("shot", None, "gx", "gy", None),
        P(None, "shot"),
        P(None, "shot"),
        P("shot", None, None),
        P("shot", None, None),
    )
    out_specs = (P("shot", "gx", "gy"), P(), P())
    return jax.shard_map(body, mesh=mesh, in_specs=in_specs, out_specs=out_specs, check_vma=False)
```

profile of v0, /device:TPU:0, one launch (start us, length us, event | category | flops | bytes accessed | tf_op | source)
XLA Modules:
  0.0 370.2 jit_solution(17085943684543270808)
XLA Ops:
  8.9 5.6 %collective-permute-start = (f32[4,32,128]{2,1,0:T(8,128)}, f32[4,32,128]{2,1,0:T(8,128)}, u32[]{:S(2)}, u32[]{:S(2)}) collective-permute-start(f32[4,32,128]{2,1,0:T(8,128)} %get-tuple-element.116), channel_id=1, source_target_pairs={{0,2},{2,4},{4,6},{1,3},{3,5},{5,7},{8,10},{10,12},{12,14},{9,11},... | collective-permute-start | bytes 196616 | tf_op jit(solution)/shard_map/while/body/eval_jaxpr/ppermute | solution.py:16
  16.1 4.0 %collective-permute-start.10 = (f32[24,8,128]{2,1,0:T(8,128)}, f32[24,8,128]{2,1,0:T(8,128)}, u32[]{:S(2)}, u32[]{:S(2)}) collective-permute-start(f32[24,8,128]{2,1,0:T(8,128)} %get-tuple-element.146), channel_id=1, source_target_pairs={{0,1},{2,3},{4,5},{6,7},{8,9},{10,11},{12,13},{14,15},{16,17},{18,... | collective-permute-start | bytes 294920 | tf_op jit(solution)/shard_map/while/body/eval_jaxpr/ppermute | solution.py:16
  21.4 1.9 slice_bitcast_fusion.3
  24.0 5.2 %collective-permute-start.6 = (f32[24,4,128]{2,1,0:T(4,128)}, f32[24,4,128]{2,1,0:T(4,128)S(1)}, u32[]{:S(2)}, u32[]{:S(2)}) collective-permute-start(f32[24,4,128]{2,1,0:T(4,128)} %get-tuple-element.152), channel_id=1, source_target_pairs={{0,1},{2,3},{4,5},{6,7},{8,9},{10,11},{12,13},{14,15},{16,17},{18,... | collective-permute-start | bytes 147464 | tf_op jit(solution)/shard_map/while/body/eval_jaxpr/ppermute | solution.py:16
  35.6 3.1 reshape.228
  38.7 4.9 %copy.58 = f32[8,6,8,2,4,4,4]{0,2,6,5,4,1,3:T(8,128)} copy(f32[8,6,8,2,4,4,4]{2,1,0,6,5,4,3:T(8,128)} %reshape.228) | data formatting | bytes 393216 | tf_op jit(solution)/shard_map/reshape | solution.py:89
  43.6 3.9 %fusion.4 = (f32[1,6,4,8,4,8,4]{5,3,6,4,2,1,0:T(8,128)}, f32[1,6,4,8,4,8,4]{5,3,6,4,2,1,0:T(8,128)S(1)}) fusion(f32[2,6,4,8,4,8,4]{5,3,6,4,2,1,0:T(8,128)} %bitcast.157), kind=kLoop, calls=%fused_computation.91 | loop fusion | flops 147456 | bytes 393216 | tf_op jit(solution)/shard_map/div | solution.py:97
  47.5 6.9 %copy.60 = f32[1,6,4,8,4,8,4]{6,5,4,3,2,1,0:T(8,128)} copy(f32[1,6,4,8,4,8,4]{5,3,6,4,2,1,0:T(8,128)} %get-tuple-element.108) | data formatting | bytes 196608 | tf_op jit(solution)/shard_map/div | solution.py:97
  54.4 2.4 div.74
  56.8 5.9 %copy.59 = f32[1,6,4,8,4,8,4]{6,5,4,3,2,1,0:T(8,128)} copy(f32[1,6,4,8,4,8,4]{5,3,6,4,2,1,0:T(8,128)S(1)} %get-tuple-element.109) | data formatting | bytes 196608 | tf_op jit(solution)/shard_map/div | solution.py:97
  62.6 2.4 div.72
  65.6 21.9 %all_gather.3 = f32[2,24,32,128]{2,1,0,3:T(8,128)S(1)} all-gather(f32[2,24,32,32]{2,1,0,3:T(8,128)S(1)} %copy.61), channel_id=1, replica_groups=mesh['shot'=4,'gx'=4,'gy'=2] {'shot'}, dimensions={3}, use_global_device_ids=true | all-gather | bytes 983040 | tf_op jit(solution)/shard_map/all_gather | solution.py:173
  87.7 1.9 fusion.394
  99.8 5.0 %fusion = f32[768,896]{1,0:T(8,128)} fusion(bf16[2048,896]{1,0:T(8,128)(2,1)S(1)} %fusion.14, s32[2048]{0:T(1024)S(1)} %bitcast.183), kind=kOutput, calls=%fused_computation.2 | convolution fusion | flops 2820145152 | bytes 6430720 | tf_op jit(solution)/shard_map/while/body/eval_jaxpr/dot_general | solution.py:149
  104.8 4.1 %reshape.226 = f32[24,32,7,128]{3,2,1,0:T(8,128)} reshape(f32[768,896]{1,0:T(8,128)} %fusion) | data formatting | bytes 5505024 | tf_op jit(solution)/shard_map/while/body/eval_jaxpr/reshape | solution.py:150
  108.9 12.5 %slice_add_fusion = (f32[24,32,1,128]{3,2,1,0:T(1,128)}, f32[24,32,1,128]{3,2,1,0:T(1,128)}, f32[24,32,1,128]{3,2,1,0:T(1,128)}, f32[24,32,1,128]{3,2,1,0:T(1,12...) fusion(f32[24,32,7,128]{3,2,1,0:T(8,128)} %reshape.226), kind=kLoop, calls=%fused_computation.478 | loop fusion | flops 98304 | bytes 5111808 | tf_op jit(solution)/shard_map/while/body/eval_jaxpr/add | solution.py:151
  122.2 1.8 copy.80
  124.8 1.8 copy.82
  129.1 5.2 %collective-permute-start.8 = (f32[24,4,128]{2,1,0:T(4,128)S(1)}, f32[24,4,128]{2,1,0:T(4,128)S(1)}, u32[]{:S(2)}, u32[]{:S(2)}) collective-permute-start(f32[24,4,128]{2,1,0:T(4,128)S(1)} %get-tuple-element.148), channel_id=1, source_target_pairs={{0,1},{2,3},{4,5},{6,7},{8,9},{10,11},{12,13},{14,15},{16,17},{18,... | collective-permute-start | bytes 147464 | tf_op jit(solution)/shard_map/ppermute | solution.py:16
  138.0 4.5 %collective-permute-start.20 = (f32[4,32,128]{2,1,0:T(8,128)}, f32[4,32,128]{2,1,0:T(8,128)S(1)}, u32[]{:S(2)}, u32[]{:S(2)}) collective-permute-start(f32[4,32,128]{2,1,0:T(8,128)} %get-tuple-element.112), channel_id=1, source_target_pairs={{0,2},{2,4},{4,6},{1,3},{3,5},{5,7},{8,10},{10,12},{12,14},{9,11},... | collective-permute-start | bytes 196616 | tf_op jit(solution)/shard_map/while/body/eval_jaxpr/ppermute | solution.py:16
  142.6 2.8 collective-permute-start.4
  149.7 3.0 collective-permute-done.5
  152.7 3.5 collective-permute-start.2
  157.5 4.7 %collective-permute-start.24 = (f32[24,4,128]{2,1,0:T(4,128)S(1)}, f32[24,4,128]{2,1,0:T(4,128)S(1)}, u32[]{:S(2)}, u32[]{:S(2)}) collective-permute-start(f32[24,4,128]{2,1,0:T(4,128)S(1)} %copy-done.19), channel_id=1, source_target_pairs={{0,1},{2,3},{4,5},{6,7},{8,9},{10,11},{12,13},{14,15},{16,17},{18,... | collective-permute-start | bytes 147464 | tf_op jit(solution)/shard_map/while/body/eval_jaxpr/ppermute | solution.py:16
  169.2 4.5 %collective-permute-start.12 = (f32[8,32,128]{2,1,0:T(8,128)S(1)}, f32[8,32,128]{2,1,0:T(8,128)S(1)}, u32[]{:S(2)}, u32[]{:S(2)}) collective-permute-start(f32[8,32,128]{2,1,0:T(8,128)S(1)} %get-tuple-element.140), channel_id=1, source_target_pairs={{0,2},{2,4},{4,6},{1,3},{3,5},{5,7},{8,10},{10,12},{12,14},{9,11},... | collective-permute-start | bytes 393224 | tf_op jit(solution)/shard_map/while/body/eval_jaxpr/ppermute | solution.py:16
  176.3 4.8 %collective-permute-done.13 = f32[8,32,128]{2,1,0:T(8,128)S(1)} collective-permute-done((f32[8,32,128]{2,1,0:T(8,128)S(1)}, f32[8,32,128]{2,1,0:T(8,128)S(1)}, u32[]{:S(2)}, u32[]{:S(2)}) %collective-permute-start.13) | collective-permute-done | bytes 131104 | tf_op jit(solution)/shard_map/while/body/eval_jaxpr/ppermute | solution.py:19
  183.6 3.9 %collective-permute-start.18 = (f32[24,8,128]{2,1,0:T(8,128)S(1)}, f32[24,8,128]{2,1,0:T(8,128)S(1)}, u32[]{:S(2)}, u32[]{:S(2)}) collective-permute-start(f32[24,8,128]{2,1,0:T(8,128)S(1)} %get-tuple-element.138), channel_id=1, source_target_pairs={{0,1},{2,3},{4,5},{6,7},{8,9},{10,11},{12,13},{14,15},{16,17},{18,... | collective-permute-start | bytes 294920 | tf_op jit(solution)/shard_map/while/body/eval_jaxpr/ppermute | solution.py:16
  189.7 2.7 collective-permute-start.16
  195.9 5.0 %collective-permute-done.17 = f32[8,32,128]{2,1,0:T(8,128)S(1)} collective-permute-done((f32[8,32,128]{2,1,0:T(8,128)S(1)}, f32[8,32,128]{2,1,0:T(8,128)S(1)}, u32[]{:S(2)}, u32[]{:S(2)}) %collective-permute-start.17) | collective-permute-done | bytes 131104 | tf_op jit(solution)/shard_map/while/body/eval_jaxpr/ppermute | solution.py:19
  205.6 2.7 collective-permute-start.26
  211.8 3.0 collective-permute-done.27
  214.8 3.5 collective-permute-start.22
  220.8 4.6 %collective-permute-done.23 = f32[8,32,128]{2,1,0:T(8,128)S(1)} collective-permute-done((f32[8,32,128]{2,1,0:T(8,128)S(1)}, f32[8,32,128]{2,1,0:T(8,128)S(1)}, u32[]{:S(2)}, u32[]{:S(2)}) %collective-permute-start.23) | collective-permute-done | bytes 131104 | tf_op jit(solution)/shard_map/while/body/eval_jaxpr/ppermute | solution.py:19
  231.0 1.9 collective-permute-start.28
  234.2 1.9 collective-permute-done.31
  236.7 3.1 collective-permute-done.29
  241.7 4.6 %collective-permute-start.34 = (f32[24,8,128]{2,1,0:T(8,128)S(1)}, f32[24,8,128]{2,1,0:T(8,128)S(1)}, u32[]{:S(2)}, u32[]{:S(2)}) collective-permute-start(f32[24,8,128]{2,1,0:T(8,128)S(1)} %get-tuple-element.124), channel_id=1, source_target_pairs={{0,1},{2,3},{4,5},{6,7},{8,9},{10,11},{12,13},{14,15},{16,17},{18,... | collective-permute-start | bytes 294920 | tf_op jit(solution)/shard_map/while/body/eval_jaxpr/ppermute | solution.py:16
  247.6 1.9 collective-permute-start.32
  253.3 3.1 collective-permute-done.33
  258.5 2.2 copy.76
  260.7 3.4 reshape.234
  264.2 21.8 %reduce-scatter.4.cloned.1.call-done = f32[32,1536]{1,0:T(8,128)} async-done(((f32[128,1536]{1,0:T(8,128)}), f32[32,1536]{1,0:T(8,128)}) %reduce-scatter.4.cloned.1.call-update) | async-done | bytes 196624
  287.8 2.7 stack.27
  290.5 2.7 stack.28
  293.2 6.8 %maximum_bitcast_fusion = f32[8,6,8,2,4,4,4]{6,0,5,2,4,1,3:T(8,128)} fusion(f32[1,6,4,8,4,8,4]{6,5,4,3,2,1,0:T(8,128)} %stack.28, f32[1,6,4,8,4,8,4]{6,5,4,3,2,1,0:T(8,128)} %stack.27), kind=kLoop, calls=%fused_computation | loop fusion | flops 49152 | bytes 393216 | tf_op jit(solution)/shard_map/transpose | solution.py:118
  300.0 17.0 %copy.70 = f32[8,6,8,2,4,4,4]{2,1,0,6,5,4,3:T(8,128)} copy(f32[8,6,8,2,4,4,4]{6,0,5,2,4,1,3:T(8,128)} %maximum_bitcast_fusion) | data formatting | bytes 393216 | tf_op jit(solution)/shard_map/transpose | solution.py:118
  316.9 2.9 reshape.229
  321.3 40.3 %all-reduce.12 = (f32[64,64]{0,1:T(8,128)S(1)}, f32[64,128]{1,0:T(8,128)}) all-reduce(f32[64,64]{0,1:T(8,128)S(1)} %convolution_bitcast_fusion, f32[64,128]{1,0:T(8,128)S(1)} %fusion.417), channel_id=1, replica_groups=mesh['shot'=4,'gx'=4,'gy'=2] {'shot','gx','gy'}, use_global_device_ids=true, to_apply=%region_1.2 | all-reduce | flops 12288 | bytes 98304 | tf_op jit(solution)/shard_map/psum | solution.py:238
  (190 shorter events, 83.6 us)
Async XLA Ops:
  7.2 28.1 %copy-start = (f32[64,128]{1,0:T(8,128)S(1)}, f32[64,128]{1,0:T(8,128)}, u32[]{:S(2)}) copy-start(f32[64,128]{1,0:T(8,128)} %param.13) | copy-start | bytes 98308
  7.2 26.5 %copy-start.10 = (f32[1,3,24,32,128]{4,3,2,1,0:T(8,128)S(1)}, f32[1,3,24,32,128]{4,3,2,1,0:T(8,128)}, u32[]{:S(2)}) copy-start(f32[1,3,24,32,128]{4,3,2,1,0:T(8,128)} %param.17) | copy-start | bytes 3538948
  7.2 27.5 %copy-start.14 = (f32[8,6,512]{2,0,1:T(8,128)S(1)}, f32[8,6,512]{2,0,1:T(8,128)}, u32[]{:S(2)}) copy-start(f32[8,6,512]{2,0,1:T(8,128)} %param.11) | copy-start | bytes 294916
  7.2 27.6 %copy-start.12 = (f32[64,64]{1,0:T(8,128)S(1)}, f32[64,64]{1,0:T(8,128)}, u32[]{:S(2)}) copy-start(f32[64,64]{1,0:T(8,128)} %param.12) | copy-start | bytes 49156
  7.2 278.8 %reduce-scatter.4.cloned.1.call-start = ((), (), s32[]{:S(2)}) async-start(), calls=%async_computation.1 | async-start | bytes 983040
  8.9 147.3 %collective-permute-start = (f32[4,32,128]{2,1,0:T(8,128)}, f32[4,32,128]{2,1,0:T(8,128)}, u32[]{:S(2)}, u32[]{:S(2)}) collective-permute-start(f32[4,32,128]{2,1,0:T(8,128)} %get-tuple-element.116), channel_id=1, source_target_pairs={{0,2},{2,4},{4,6},{1,3},{3,5},{5,7},{8,10},{10,12},{12,14},{9,11},... | collective-permute-start | bytes 196616 | tf_op jit(solution)/shard_map/while/body/eval_jaxpr/ppermute | solution.py:16
  16.1 112.9 %collective-permute-start.10 = (f32[24,8,128]{2,1,0:T(8,128)}, f32[24,8,128]{2,1,0:T(8,128)}, u32[]{:S(2)}, u32[]{:S(2)}) collective-permute-start(f32[24,8,128]{2,1,0:T(8,128)} %get-tuple-element.146), channel_id=1, source_target_pairs={{0,1},{2,3},{4,5},{6,7},{8,9},{10,11},{12,13},{14,15},{16,17},{18,... | collective-permute-start | bytes 294920 | tf_op jit(solution)/shard_map/while/body/eval_jaxpr/ppermute | solution.py:16
  20.1 114.1 %collective-permute-start.11 = (f32[24,8,128]{2,1,0:T(8,128)}, f32[24,8,128]{2,1,0:T(8,128)}, u32[]{:S(2)}, u32[]{:S(2)}) collective-permute-start(f32[24,8,128]{2,1,0:T(8,128)} %get-tuple-element.147), channel_id=1, source_target_pairs={{1,0},{3,2},{5,4},{7,6},{9,8},{11,10},{13,12},{15,14},{17,16},{19,... | collective-permute-start | bytes 294920 | tf_op jit(solution)/shard_map/while/body/eval_jaxpr/ppermute | solution.py:19
  24.0 112.5 %collective-permute-start.6 = (f32[24,4,128]{2,1,0:T(4,128)}, f32[24,4,128]{2,1,0:T(4,128)S(1)}, u32[]{:S(2)}, u32[]{:S(2)}) collective-permute-start(f32[24,4,128]{2,1,0:T(4,128)} %get-tuple-element.152), channel_id=1, source_target_pairs={{0,1},{2,3},{4,5},{6,7},{8,9},{10,11},{12,13},{14,15},{16,17},{18,... | collective-permute-start | bytes 147464 | tf_op jit(solution)/shard_map/while/body/eval_jaxpr/ppermute | solution.py:16
  29.2 108.8 %collective-permute-start.7 = (f32[24,4,128]{2,1,0:T(4,128)}, f32[24,4,128]{2,1,0:T(4,128)}, u32[]{:S(2)}, u32[]{:S(2)}) collective-permute-start(f32[24,4,128]{2,1,0:T(4,128)} %get-tuple-element.153), channel_id=1, source_target_pairs={{1,0},{3,2},{5,4},{7,6},{9,8},{11,10},{13,12},{15,14},{17,16},{19,... | collective-permute-start | bytes 147464 | tf_op jit(solution)/shard_map/while/body/eval_jaxpr/ppermute | solution.py:19
  124.0 18.6 %copy-start.13 = (f32[8,32,128]{2,1,0:T(8,128)S(1)}, f32[8,32,128]{2,1,0:T(8,128)}, u32[]{:S(2)}) copy-start(f32[8,32,128]{2,1,0:T(8,128)} %get-tuple-element.144) | copy-start | bytes 393220
  129.1 13.5 %collective-permute-start.8 = (f32[24,4,128]{2,1,0:T(4,128)S(1)}, f32[24,4,128]{2,1,0:T(4,128)S(1)}, u32[]{:S(2)}, u32[]{:S(2)}) collective-permute-start(f32[24,4,128]{2,1,0:T(4,128)S(1)} %get-tuple-element.148), channel_id=1, source_target_pairs={{0,1},{2,3},{4,5},{6,7},{8,9},{10,11},{12,13},{14,15},{16,17},{18,... | collective-permute-start | bytes 147464 | tf_op jit(solution)/shard_map/ppermute | solution.py:16
  134.2 11.2 %collective-permute-start.9 = (f32[24,4,128]{2,1,0:T(4,128)S(1)}, f32[24,4,128]{2,1,0:T(4,128)S(1)}, u32[]{:S(2)}, u32[]{:S(2)}) collective-permute-start(f32[24,4,128]{2,1,0:T(4,128)S(1)} %get-tuple-element.149), channel_id=1, source_target_pairs={{1,0},{3,2},{5,4},{7,6},{9,8},{11,10},{13,12},{15,14},{17,16},{19,... | collective-permute-start | bytes 147464 | tf_op jit(solution)/shard_map/ppermute | solution.py:19
  136.5 11.9 %copy-start.16 = (f32[1,4,32,128]{3,2,1,0:T(8,128)S(1)}, f32[1,4,32,128]{3,2,1,0:T(8,128)}, u32[]{:S(2)}) copy-start(f32[1,4,32,128]{3,2,1,0:T(8,128)} %copy.83) | copy-start | bytes 196612
  136.5 16.1 %copy-start.15 = (f32[1,4,32,128]{3,2,1,0:T(8,128)S(1)}, f32[1,4,32,128]{3,2,1,0:T(8,128)}, u32[]{:S(2)}) copy-start(f32[1,4,32,128]{3,2,1,0:T(8,128)} %copy.81) | copy-start | bytes 196612
  136.5 21.0 %collective-permute-start.1 = (f32[4,32,128]{2,1,0:T(8,128)}, f32[4,32,128]{2,1,0:T(8,128)S(1)}, u32[]{:S(2)}, u32[]{:S(2)}) collective-permute-start(f32[4,32,128]{2,1,0:T(8,128)} %get-tuple-element.117), channel_id=1, source_target_pairs={{2,0},{4,2},{6,4},{3,1},{5,3},{7,5},{10,8},{12,10},{14,12},{11,9},... | collective-permute-start | bytes 196616 | tf_op jit(solution)/shard_map/while/body/eval_jaxpr/ppermute | solution.py:19
  138.0 87.4 %collective-permute-start.20 = (f32[4,32,128]{2,1,0:T(8,128)}, f32[4,32,128]{2,1,0:T(8,128)S(1)}, u32[]{:S(2)}, u32[]{:S(2)}) collective-permute-start(f32[4,32,128]{2,1,0:T(8,128)} %get-tuple-element.112), channel_id=1, source_target_pairs={{0,2},{2,4},{4,6},{1,3},{3,5},{5,7},{8,10},{10,12},{12,14},{9,11},... | collective-permute-start | bytes 196616 | tf_op jit(solution)/shard_map/while/body/eval_jaxpr/ppermute | solution.py:16
  142.6 5.8 %collective-permute-start.4 = (f32[8,32,128]{2,1,0:T(8,128)S(1)}, f32[8,32,128]{2,1,0:T(8,128)S(1)}, u32[]{:S(2)}, u32[]{:S(2)}) collective-permute-start(f32[8,32,128]{2,1,0:T(8,128)S(1)} %copy-done.13), channel_id=1, source_target_pairs={{0,2},{2,4},{4,6},{1,3},{3,5},{5,7},{8,10},{10,12},{12,14},{9,11},... | collective-permute-start | bytes 393224 | tf_op jit(solution)/shard_map/while/body/eval_jaxpr/ppermute | solution.py:16
  145.4 10.8 %copy-start.17 = (f32[4,32,128]{2,1,0:T(8,128)S(1)}, f32[4,32,128]{2,1,0:T(8,128)}, u32[]{:S(2)}) copy-start(f32[4,32,128]{2,1,0:T(8,128)} %get-tuple-element.113) | copy-start | bytes 196612
  145.4 12.1 %copy-start.19 = (f32[24,4,128]{2,1,0:T(4,128)S(1)}, f32[24,4,128]{2,1,0:T(4,128)}, u32[]{:S(2)}) copy-start(f32[24,4,128]{2,1,0:T(4,128)} %get-tuple-element.132) | copy-start | bytes 147460
  145.4 16.8 %copy-start.7 = (f32[24,32,128]{2,1,0:T(8,128)S(1)}, f32[24,32,128]{2,1,0:T(8,128)}, u32[]{:S(2)}) copy-start(f32[24,32,128]{2,1,0:T(8,128)} %get-tuple-element.118) | copy-start | bytes 1179652
  145.5 7.2 %collective-permute-start.5 = (f32[8,32,128]{2,1,0:T(8,128)}, f32[8,32,128]{2,1,0:T(8,128)S(1)}, u32[]{:S(2)}, u32[]{:S(2)}) collective-permute-start(f32[8,32,128]{2,1,0:T(8,128)} %get-tuple-element.145), channel_id=1, source_target_pairs={{2,0},{4,2},{6,4},{3,1},{5,3},{7,5},{10,8},{12,10},{14,12},{11,9},... | collective-permute-start | bytes 393224 | tf_op jit(solution)/shard_map/while/body/eval_jaxpr/ppermute | solution.py:19
  148.4 13.9 %collective-permute-start.3 = (f32[4,32,128]{2,1,0:T(8,128)S(1)}, f32[4,32,128]{2,1,0:T(8,128)S(1)}, u32[]{:S(2)}, u32[]{:S(2)}) collective-permute-start(f32[4,32,128]{2,1,0:T(8,128)S(1)} %bitcast.176), channel_id=1, source_target_pairs={{2,0},{4,2},{6,4},{3,1},{5,3},{7,5},{10,8},{12,10},{14,12},{11,9},... | collective-permute-start | bytes 196616 | tf_op jit(solution)/shard_map/ppermute | solution.py:19
  152.7 9.6 %collective-permute-start.2 = (f32[4,32,128]{2,1,0:T(8,128)S(1)}, f32[4,32,128]{2,1,0:T(8,128)S(1)}, u32[]{:S(2)}, u32[]{:S(2)}) collective-permute-start(f32[4,32,128]{2,1,0:T(8,128)S(1)} %bitcast.175), channel_id=1, source_target_pairs={{0,2},{2,4},{4,6},{1,3},{3,5},{5,7},{8,10},{10,12},{12,14},{9,11},... | collective-permute-start | bytes 196616 | tf_op jit(solution)/shard_map/ppermute | solution.py:16
  156.2 69.2 %collective-permute-start.21 = (f32[4,32,128]{2,1,0:T(8,128)S(1)}, f32[4,32,128]{2,1,0:T(8,128)S(1)}, u32[]{:S(2)}, u32[]{:S(2)}) collective-permute-start(f32[4,32,128]{2,1,0:T(8,128)S(1)} %copy-done.17), channel_id=1, source_target_pairs={{2,0},{4,2},{6,4},{3,1},{5,3},{7,5},{10,8},{12,10},{14,12},{11,9},... | collective-permute-start | bytes 196616 | tf_op jit(solution)/shard_map/while/body/eval_jaxpr/ppermute | solution.py:19
  157.5 60.8 %collective-permute-start.24 = (f32[24,4,128]{2,1,0:T(4,128)S(1)}, f32[24,4,128]{2,1,0:T(4,128)S(1)}, u32[]{:S(2)}, u32[]{:S(2)}) collective-permute-start(f32[24,4,128]{2,1,0:T(4,128)S(1)} %copy-done.19), channel_id=1, source_target_pairs={{0,1},{2,3},{4,5},{6,7},{8,9},{10,11},{12,13},{14,15},{16,17},{18,... | collective-permute-start | bytes 147464 | tf_op jit(solution)/shard_map/while/body/eval_jaxpr/ppermute | solution.py:16
  165.7 3.5 collective-permute-start.14
  167.0 6.7 %collective-permute-start.15 = (f32[24,8,128]{2,1,0:T(8,128)S(1)}, f32[24,8,128]{2,1,0:T(8,128)S(1)}, u32[]{:S(2)}, u32[]{:S(2)}) collective-permute-start(f32[24,8,128]{2,1,0:T(8,128)S(1)} %get-tuple-element.143), channel_id=1, source_target_pairs={{1,0},{3,2},{5,4},{7,6},{9,8},{11,10},{13,12},{15,14},{17,16},{19,... | collective-permute-start | bytes 294920 | tf_op jit(solution)/shard_map/while/body/eval_jaxpr/ppermute | solution.py:19
  169.2 7.0 %collective-permute-start.12 = (f32[8,32,128]{2,1,0:T(8,128)S(1)}, f32[8,32,128]{2,1,0:T(8,128)S(1)}, u32[]{:S(2)}, u32[]{:S(2)}) collective-permute-start(f32[8,32,128]{2,1,0:T(8,128)S(1)} %get-tuple-element.140), channel_id=1, source_target_pairs={{0,2},{2,4},{4,6},{1,3},{3,5},{5,7},{8,10},{10,12},{12,14},{9,11},... | collective-permute-start | bytes 393224 | tf_op jit(solution)/shard_map/while/body/eval_jaxpr/ppermute | solution.py:16
  173.8 7.2 %collective-permute-start.13 = (f32[8,32,128]{2,1,0:T(8,128)S(1)}, f32[8,32,128]{2,1,0:T(8,128)S(1)}, u32[]{:S(2)}, u32[]{:S(2)}) collective-permute-start(f32[8,32,128]{2,1,0:T(8,128)S(1)} %get-tuple-element.141), channel_id=1, source_target_pairs={{2,0},{4,2},{6,4},{3,1},{5,3},{7,5},{10,8},{12,10},{14,12},{11,9},... | collective-permute-start | bytes 393224 | tf_op jit(solution)/shard_map/while/body/eval_jaxpr/ppermute | solution.py:19
  183.6 6.1 %collective-permute-start.18 = (f32[24,8,128]{2,1,0:T(8,128)S(1)}, f32[24,8,128]{2,1,0:T(8,128)S(1)}, u32[]{:S(2)}, u32[]{:S(2)}) collective-permute-start(f32[24,8,128]{2,1,0:T(8,128)S(1)} %get-tuple-element.138), channel_id=1, source_target_pairs={{0,1},{2,3},{4,5},{6,7},{8,9},{10,11},{12,13},{14,15},{16,17},{18,... | collective-permute-start | bytes 294920 | tf_op jit(solution)/shard_map/while/body/eval_jaxpr/ppermute | solution.py:16
  187.5 6.5 %collective-permute-start.19 = (f32[24,8,128]{2,1,0:T(8,128)S(1)}, f32[24,8,128]{2,1,0:T(8,128)S(1)}, u32[]{:S(2)}, u32[]{:S(2)}) collective-permute-start(f32[24,8,128]{2,1,0:T(8,128)S(1)} %get-tuple-element.139), channel_id=1, source_target_pairs={{1,0},{3,2},{5,4},{7,6},{9,8},{11,10},{13,12},{15,14},{17,16},{19,... | collective-permute-start | bytes 294920 | tf_op jit(solution)/shard_map/while/body/eval_jaxpr/ppermute | solution.py:19
  189.7 6.2 %collective-permute-start.16 = (f32[8,32,128]{2,1,0:T(8,128)S(1)}, f32[8,32,128]{2,1,0:T(8,128)S(1)}, u32[]{:S(2)}, u32[]{:S(2)}) collective-permute-start(f32[8,32,128]{2,1,0:T(8,128)S(1)} %get-tuple-element.136), channel_id=1, source_target_pairs={{0,2},{2,4},{4,6},{1,3},{3,5},{5,7},{8,10},{10,12},{12,14},{9,11},... | collective-permute-start | bytes 393224 | tf_op jit(solution)/shard_map/while/body/eval_jaxpr/ppermute | solution.py:16
  194.0 6.8 %collective-permute-start.17 = (f32[8,32,128]{2,1,0:T(8,128)S(1)}, f32[8,32,128]{2,1,0:T(8,128)S(1)}, u32[]{:S(2)}, u32[]{:S(2)}) collective-permute-start(f32[8,32,128]{2,1,0:T(8,128)S(1)} %get-tuple-element.137), channel_id=1, source_target_pairs={{2,0},{4,2},{6,4},{3,1},{5,3},{7,5},{10,8},{12,10},{14,12},{11,9},... | collective-permute-start | bytes 393224 | tf_op jit(solution)/shard_map/while/body/eval_jaxpr/ppermute | solution.py:19
  203.7 16.1 %copy-start.2 = (f32[24,32,128]{2,1,0:T(8,128)S(1)}, f32[24,32,128]{2,1,0:T(8,128)}, u32[]{:S(2)}) copy-start(f32[24,32,128]{2,1,0:T(8,128)} %get-tuple-element.115) | copy-start | bytes 1179652
  205.6 4.9 %collective-permute-start.26 = (f32[24,8,128]{2,1,0:T(8,128)S(1)}, f32[24,8,128]{2,1,0:T(8,128)S(1)}, u32[]{:S(2)}, u32[]{:S(2)}) collective-permute-start(f32[24,8,128]{2,1,0:T(8,128)S(1)} %get-tuple-element.134), channel_id=1, source_target_pairs={{0,1},{2,3},{4,5},{6,7},{8,9},{10,11},{12,13},{14,15},{16,17},{18,... | collective-permute-start | bytes 294920 | tf_op jit(solution)/shard_map/while/body/eval_jaxpr/ppermute | solution.py:16
  208.3 6.5 %collective-permute-start.27 = (f32[24,8,128]{2,1,0:T(8,128)S(1)}, f32[24,8,128]{2,1,0:T(8,128)S(1)}, u32[]{:S(2)}, u32[]{:S(2)}) collective-permute-start(f32[24,8,128]{2,1,0:T(8,128)S(1)} %get-tuple-element.135), channel_id=1, source_target_pairs={{1,0},{3,2},{5,4},{7,6},{9,8},{11,10},{13,12},{15,14},{17,16},{19,... | collective-permute-start | bytes 294920 | tf_op jit(solution)/shard_map/while/body/eval_jaxpr/ppermute | solution.py:19
  210.5 9.3 %collective-permute-start.25 = (f32[24,4,128]{2,1,0:T(4,128)S(1)}, f32[24,4,128]{2,1,0:T(4,128)S(1)}, u32[]{:S(2)}, u32[]{:S(2)}) collective-permute-start(f32[24,4,128]{2,1,0:T(4,128)S(1)} %copy-done.18), channel_id=1, source_target_pairs={{1,0},{3,2},{5,4},{7,6},{9,8},{11,10},{13,12},{15,14},{17,16},{19,... | collective-permute-start | bytes 147464 | tf_op jit(solution)/shard_map/while/body/eval_jaxpr/ppermute | solution.py:19
  214.8 6.0 %collective-permute-start.22 = (f32[8,32,128]{2,1,0:T(8,128)S(1)}, f32[8,32,128]{2,1,0:T(8,128)S(1)}, u32[]{:S(2)}, u32[]{:S(2)}) collective-permute-start(f32[8,32,128]{2,1,0:T(8,128)S(1)} %get-tuple-element.130), channel_id=1, source_target_pairs={{0,2},{2,4},{4,6},{1,3},{3,5},{5,7},{8,10},{10,12},{12,14},{9,11},... | collective-permute-start | bytes 393224 | tf_op jit(solution)/shard_map/while/body/eval_jaxpr/ppermute | solution.py:16
  218.3 7.0 %collective-permute-start.23 = (f32[8,32,128]{2,1,0:T(8,128)S(1)}, f32[8,32,128]{2,1,0:T(8,128)S(1)}, u32[]{:S(2)}, u32[]{:S(2)}) collective-permute-start(f32[8,32,128]{2,1,0:T(8,128)S(1)} %get-tuple-element.131), channel_id=1, source_target_pairs={{2,0},{4,2},{6,4},{3,1},{5,3},{7,5},{10,8},{12,10},{14,12},{11,9},... | collective-permute-start | bytes 393224 | tf_op jit(solution)/shard_map/while/body/eval_jaxpr/ppermute | solution.py:19
  228.1 6.1 %collective-permute-start.30 = (f32[24,8,128]{2,1,0:T(8,128)S(1)}, f32[24,8,128]{2,1,0:T(8,128)S(1)}, u32[]{:S(2)}, u32[]{:S(2)}) collective-permute-start(f32[24,8,128]{2,1,0:T(8,128)S(1)} %get-tuple-element.128), channel_id=1, source_target_pairs={{0,1},{2,3},{4,5},{6,7},{8,9},{10,11},{12,13},{14,15},{16,17},{18,... | collective-permute-start | bytes 294920 | tf_op jit(solution)/shard_map/while/body/eval_jaxpr/ppermute | solution.py:16
  229.7 6.5 %collective-permute-start.31 = (f32[24,8,128]{2,1,0:T(8,128)S(1)}, f32[24,8,128]{2,1,0:T(8,128)S(1)}, u32[]{:S(2)}, u32[]{:S(2)}) collective-permute-start(f32[24,8,128]{2,1,0:T(8,128)S(1)} %get-tuple-element.129), channel_id=1, source_target_pairs={{1,0},{3,2},{5,4},{7,6},{9,8},{11,10},{13,12},{15,14},{17,16},{19,... | collective-permute-start | bytes 294920 | tf_op jit(solution)/shard_map/while/body/eval_jaxpr/ppermute | solution.py:19
  231.0 5.7 %collective-permute-start.28 = (f32[8,32,128]{2,1,0:T(8,128)S(1)}, f32[8,32,128]{2,1,0:T(8,128)S(1)}, u32[]{:S(2)}, u32[]{:S(2)}) collective-permute-start(f32[8,32,128]{2,1,0:T(8,128)S(1)} %get-tuple-element.126), channel_id=1, source_target_pairs={{0,2},{2,4},{4,6},{1,3},{3,5},{5,7},{8,10},{10,12},{12,14},{9,11},... | collective-permute-start | bytes 393224 | tf_op jit(solution)/shard_map/while/body/eval_jaxpr/ppermute | solution.py:16
  232.9 6.9 %collective-permute-start.29 = (f32[8,32,128]{2,1,0:T(8,128)S(1)}, f32[8,32,128]{2,1,0:T(8,128)S(1)}, u32[]{:S(2)}, u32[]{:S(2)}) collective-permute-start(f32[8,32,128]{2,1,0:T(8,128)S(1)} %get-tuple-element.127), channel_id=1, source_target_pairs={{2,0},{4,2},{6,4},{3,1},{5,3},{7,5},{10,8},{12,10},{14,12},{11,9},... | collective-permute-start | bytes 393224 | tf_op jit(solution)/shard_map/while/body/eval_jaxpr/ppermute | solution.py:19
  241.7 9.3 %collective-permute-start.34 = (f32[24,8,128]{2,1,0:T(8,128)S(1)}, f32[24,8,128]{2,1,0:T(8,128)S(1)}, u32[]{:S(2)}, u32[]{:S(2)}) collective-permute-start(f32[24,8,128]{2,1,0:T(8,128)S(1)} %get-tuple-element.124), channel_id=1, source_target_pairs={{0,1},{2,3},{4,5},{6,7},{8,9},{10,11},{12,13},{14,15},{16,17},{18,... | collective-permute-start | bytes 294920 | tf_op jit(solution)/shard_map/while/body/eval_jaxpr/ppermute | solution.py:16
  246.2 6.5 %collective-permute-start.35 = (f32[24,8,128]{2,1,0:T(8,128)S(1)}, f32[24,8,128]{2,1,0:T(8,128)S(1)}, u32[]{:S(2)}, u32[]{:S(2)}) collective-permute-start(f32[24,8,128]{2,1,0:T(8,128)S(1)} %get-tuple-element.125), channel_id=1, source_target_pairs={{1,0},{3,2},{5,4},{7,6},{9,8},{11,10},{13,12},{15,14},{17,16},{19,... | collective-permute-start | bytes 294920 | tf_op jit(solution)/shard_map/while/body/eval_jaxpr/ppermute | solution.py:19
  247.6 5.7 %collective-permute-start.32 = (f32[8,32,128]{2,1,0:T(8,128)S(1)}, f32[8,32,128]{2,1,0:T(8,128)S(1)}, u32[]{:S(2)}, u32[]{:S(2)}) collective-permute-start(f32[8,32,128]{2,1,0:T(8,128)S(1)} %get-tuple-element.122), channel_id=1, source_target_pairs={{0,2},{2,4},{4,6},{1,3},{3,5},{5,7},{8,10},{10,12},{12,14},{9,11},... | collective-permute-start | bytes 393224 | tf_op jit(solution)/shard_map/while/body/eval_jaxpr/ppermute | solution.py:16
  249.5 6.9 %collective-permute-start.33 = (f32[8,32,128]{2,1,0:T(8,128)S(1)}, f32[8,32,128]{2,1,0:T(8,128)S(1)}, u32[]{:S(2)}, u32[]{:S(2)}) collective-permute-start(f32[8,32,128]{2,1,0:T(8,128)S(1)} %get-tuple-element.123), channel_id=1, source_target_pairs={{2,0},{4,2},{6,4},{3,1},{5,3},{7,5},{10,8},{12,10},{14,12},{11,9},... | collective-permute-start | bytes 393224 | tf_op jit(solution)/shard_map/while/body/eval_jaxpr/ppermute | solution.py:19
  (13 other events, 41.9 us)
Sparse Core Ops, SparseCore 0:
  264.3 21.5 reduce-scatter.3
where the time goes:
time: 377 us; the launch traced here: 370 us
  starting transfers between devices  87.9 us (23%)
  local copies, waits for them, and re-layouts  87 us (23%)
  blocking collectives  62.2 us (16%)
  waiting for transfers between devices  57.2 us (15%)
  other arithmetic  51.9 us (14%)
  between operations  16.7 us (4%)
  matrix products  7.16 us (2%)
    ppermute x18, starting transfers between devices, with_halo(): lax.ppermute(lax.slice_in_dim(block, block.shape[dim] - width, None, axis...  64.1 us
    psum x1, blocking collectives, body(): lax.psum((grad_first, grad_second), ('shot', 'gx', 'gy'))  40.3 us
    ppermute x18, waiting for transfers between devices, with_halo(): lax.ppermute(lax.slice_in_dim(block, 0, width, axis=dim), axis, backward)  31.8 us
    ppermute x18, starting transfers between devices, with_halo(): lax.ppermute(lax.slice_in_dim(block, 0, width, axis=dim), axis, backward)  23.8 us
    all_gather x1, blocking collectives, body(): lax.all_gather(jnp.stack([slab_mod, slab_buoy]), 'shot', axis=3, tiled=True)  21.9 us
    unnamed x2, waiting for transfers between devices  21.8 us
    div x4, local copies, waits for them, and re-layouts, materials(): wave_speed = 0.15 + 0.25 * jax.nn.sigmoid(fine_out[0])  17.6 us
    transpose x1, local copies, waits for them, and re-layouts, decoder_grads(): grad_out = grad_fine.reshape(2, size_x // 4, 4, size_y // 4, 4, size_z //...  17 us
  transfers between devices with their start and end apart: 37, of which 16 were waited for; matrix products, arithmetic and copies ran while one was open for 25% of the time, Pallas kernels for 0%

commit v1 on v0

--- a/solution.py
+++ b/solution.py
@@ -6,6 +6,18 @@
 CH = 64
 STEPS = 3
 coeffs = (1225.0 / 1024.0, -245.0 / 3072.0, 49.0 / 5120.0, -5.0 / 7168.0)
+
+
+def gather_by_bits(x, axis, dim):
+    ways, here, step = (lax.axis_size(axis), lax.axis_index(axis), x.shape[dim])
+    line, have = (x, 1)
+    while have < ways:
+        line = jnp.concatenate(
+            [line, lax.ppermute(line, axis, [(d, (d - have) % ways) for d in range(ways)])],
+            axis=dim,
+        )
+        have = 2 * have
+    return jnp.roll(line, here * step, axis=dim)
 
 
 def with_halo(block, sides, width):
@@ -170,7 +182,7 @@
     anchor_y = lax.axis_index("gy") * size_y
     flattened, hidden, fine_out = decode(latent, w_first, w_second)
     slab_mod, slab_buoy = materials(fine_out)
-    stacked = lax.all_gather(jnp.stack([slab_mod, slab_buoy]), "shot", axis=3, tiled=True)
+    stacked = gather_by_bits(jnp.stack([slab_mod, slab_buoy]), "shot", 3)
     modulus, buoyancy = (stacked[0], stacked[1])
     buoy_x = rim_x(buoyancy)
     buoy_y = rim_y(buoyancy)

time: 377 us -> 359 us (0.952)
  blocking collectives: 62.2 us -> 40.3 us
  starting transfers between devices: 87.9 us -> 96.4 us
  local copies, waits for them, and re-layouts: 87 us -> 78.6 us
    all_gather x1 -> x0, blocking collectives: 21.9 us -> none  [body(): lax.all_gather(jnp.stack([slab_mod, slab_buoy]), 'shot', axis=3, tiled=True)]
    ppermute x18, starting transfers between devices: 64.1 us -> 70.7 us  [with_halo(): lax.ppermute(lax.slice_in_dim(block, block.shape[dim] - width, None, axis...]
    unnamed x60, local copies, waits for them, and re-layouts: 16.4 us -> 10.7 us
    ppermute x18, waiting for transfers between devices: 31.8 us -> 27.3 us  [with_halo(): lax.ppermute(lax.slice_in_dim(block, 0, width, axis=dim), axis, backward)]
    concatenate x0 -> x1, local copies, waits for them, and re-layouts: none -> 4.09 us  [gather_by_bits(): return jnp.roll(line, here * step, axis=dim)]
  transfers between devices with their start and end apart: 37 -> 39, of which waited for: 16 -> 17; matrix products, arithmetic and copies ran while one was open for 25% -> 26% of each run, Pallas kernels for 0% -> 0%
where the time goes in v1:
time: 359 us; the launch traced here: 352 us
  starting transfers between devices  96.4 us (27%)
  local copies, waits for them, and re-layouts  78.6 us (22%)
  waiting for transfers between devices  57.5 us (16%)
  other arithmetic  54.3 us (15%)
  blocking collectives  40.3 us (11%)
  between operations  16.7 us (5%)
  matrix products  7.92 us (2%)
    ppermute x18, starting transfers between devices, with_halo(): lax.ppermute(lax.slice_in_dim(block, block.shape[dim] - width, None, axis...  70.7 us
    psum x1, blocking collectives, body(): lax.psum((grad_first, grad_second), ('shot', 'gx', 'gy'))  40.3 us
    ppermute x18, waiting for transfers between devices, with_halo(): lax.ppermute(lax.slice_in_dim(block, 0, width, axis=dim), axis, backward)  27.3 us
    ppermute x18, starting transfers between devices, with_halo(): lax.ppermute(lax.slice_in_dim(block, 0, width, axis=dim), axis, backward)  23.6 us
    unnamed x2, waiting for transfers between devices  22.8 us
    transpose x1, local copies, waits for them, and re-layouts, decoder_grads(): grad_out = grad_fine.reshape(2, size_x // 4, 4, size_y // 4, 4, size_z //...  17 us
    div x4, local copies, waits for them, and re-layouts, materials(): wave_speed = 0.15 + 0.25 * jax.nn.sigmoid(fine_out[0])  14.6 us
    add x1, other arithmetic, receiver_fields(): planes[:, :, 1 + 2 * m] + planes[:, :, 2 + 2 * m]  12.5 us
  transfers between devices with their start and end apart: 39, of which 17 were waited for; matrix products, arithmetic and copies ran while one was open for 26% of the time, Pallas kernels for 0%

profile of v1, /device:TPU:0, one launch (start us, length us, event | category | flops | bytes accessed | tf_op | source)
XLA Modules:
  0.0 351.8 jit_solution(1062184977956135061)
XLA Ops:
  8.9 5.5 %collective-permute-start.12 = (f32[24,8,128]{2,1,0:T(8,128)}, f32[24,8,128]{2,1,0:T(8,128)}, u32[]{:S(2)}, u32[]{:S(2)}) collective-permute-start(f32[24,8,128]{2,1,0:T(8,128)} %get-tuple-element.145), channel_id=1, source_target_pairs={{0,1},{2,3},{4,5},{6,7},{8,9},{10,11},{12,13},{14,15},{16,17},{18,... | collective-permute-start | bytes 294920 | tf_op jit(solution)/shard_map/while/body/eval_jaxpr/ppermute | solution.py:28
  17.3 4.1 %collective-permute-start.6 = (f32[8,32,128]{2,1,0:T(8,128)}, f32[8,32,128]{2,1,0:T(8,128)}, u32[]{:S(2)}, u32[]{:S(2)}) collective-permute-start(f32[8,32,128]{2,1,0:T(8,128)} %get-tuple-element.143), channel_id=1, source_target_pairs={{0,2},{2,4},{4,6},{1,3},{3,5},{5,7},{8,10},{10,12},{12,14},{9,11},... | collective-permute-start | bytes 393224 | tf_op jit(solution)/shard_map/while/body/eval_jaxpr/ppermute | solution.py:28
  25.4 3.1 reshape.228
  28.5 3.4 copy.53
  31.9 2.4 fusion.4
  34.3 5.7 %copy.55 = f32[1,6,4,8,4,8,4]{6,5,4,3,2,1,0:T(8,128)S(1)} copy(f32[1,6,4,8,4,8,4]{5,3,6,4,2,1,0:T(8,128)} %get-tuple-element.105) | data formatting | bytes 196608 | tf_op jit(solution)/shard_map/div | solution.py:109
  41.6 5.7 %copy.54 = f32[1,6,4,8,4,8,4]{6,5,4,3,2,1,0:T(8,128)S(1)} copy(f32[1,6,4,8,4,8,4]{5,3,6,4,2,1,0:T(8,128)} %get-tuple-element.106) | data formatting | bytes 196608 | tf_op jit(solution)/shard_map/div | solution.py:109
  52.8 1.9 slice_bitcast_fusion.3
  56.4 1.9 slice_bitcast_fusion.1
  67.6 5.0 %fusion = f32[768,896]{1,0:T(8,128)} fusion(bf16[2048,896]{1,0:T(8,128)(2,1)S(1)} %fusion.14, s32[2048]{0:T(1024)S(1)} %bitcast.156), kind=kOutput, calls=%fused_computation.2 | convolution fusion | flops 2820145152 | bytes 6430720 | tf_op jit(solution)/shard_map/while/body/eval_jaxpr/dot_general | solution.py:161
  72.6 4.1 %reshape.226 = f32[24,32,7,128]{3,2,1,0:T(8,128)} reshape(f32[768,896]{1,0:T(8,128)} %fusion) | data formatting | bytes 5505024 | tf_op jit(solution)/shard_map/while/body/eval_jaxpr/reshape | solution.py:162
  76.7 12.5 %slice_add_fusion = (f32[24,32,1,128]{3,2,1,0:T(1,128)}, f32[24,32,1,128]{3,2,1,0:T(1,128)}, f32[24,32,1,128]{3,2,1,0:T(1,128)}, f32[24,32,1,128]{3,2,1,0:T(1,12...) fusion(f32[24,32,7,128]{3,2,1,0:T(8,128)} %reshape.226), kind=kLoop, calls=%fused_computation.479 | loop fusion | flops 98304 | bytes 5111808 | tf_op jit(solution)/shard_map/while/body/eval_jaxpr/add | solution.py:163
  92.0 5.2 %collective-permute-start.2 = (f32[4,32,128]{2,1,0:T(8,128)}, f32[4,32,128]{2,1,0:T(8,128)}, u32[]{:S(2)}, u32[]{:S(2)}) collective-permute-start(f32[4,32,128]{2,1,0:T(8,128)} %get-tuple-element.115), channel_id=1, source_target_pairs={{0,2},{2,4},{4,6},{1,3},{3,5},{5,7},{8,10},{10,12},{12,14},{9,11},... | collective-permute-start | bytes 196616 | tf_op jit(solution)/shard_map/while/body/eval_jaxpr/ppermute | solution.py:28
  97.2 5.8 %collective-permute-start.8 = (f32[24,4,128]{2,1,0:T(4,128)}, f32[24,4,128]{2,1,0:T(4,128)}, u32[]{:S(2)}, u32[]{:S(2)}) collective-permute-start(f32[24,4,128]{2,1,0:T(4,128)} %get-tuple-element.151), channel_id=1, source_target_pairs={{0,1},{2,3},{4,5},{6,7},{8,9},{10,11},{12,13},{14,15},{16,17},{18,... | collective-permute-start | bytes 147464 | tf_op jit(solution)/shard_map/while/body/eval_jaxpr/ppermute | solution.py:28
  106.3 3.6 %collective-permute-done.1 = f32[2,24,32,64]{3,2,1,0:T(8,128)} collective-permute-done((f32[2,24,32,64]{3,2,1,0:T(8,128)S(1)}, f32[2,24,32,64]{3,2,1,0:T(8,128)}, u32[]{:S(2)}, u32[]{:S(2)}) %collective-permute-start.1) | collective-permute-done | bytes 393248 | tf_op jit(solution)/shard_map/ppermute | solution.py:16
  109.9 4.1 %concatenate.124 = f32[2,24,32,256]{3,2,1,0:T(8,128)S(1)} concatenate(f32[2,24,32,32]{3,2,1,0:T(8,128)} %copy-done.2, f32[2,24,32,32]{3,2,1,0:T(8,128)} %copy-done.3, f32[2,24,32,64]{3,2,1,0:T(8,128)} %collective-permute-done.1, f32[2,24,32,32]{3,2,1,0:T(8,128)} %copy-done.2, f32[2,24,32,32]{3,2,1,0:T(8,128)} %copy-done.3, f32[2,24,32,64]{3,2,1,0:T(8,128)} %collective-permute-done.1), dimensions={3} | concatenate | bytes 3145728 | tf_op jit(solution)/shard_map/jit(_roll_dynamic)/concatenate | solution.py:20
  114.0 1.9 bitcast_subtract_fusion.2
  115.9 5.3 %collective-permute-start.10 = (f32[24,4,128]{2,1,0:T(4,128)S(1)}, f32[24,4,128]{2,1,0:T(4,128)S(1)}, u32[]{:S(2)}, u32[]{:S(2)}) collective-permute-start(f32[24,4,128]{2,1,0:T(4,128)S(1)} %get-tuple-element.147), channel_id=1, source_target_pairs={{0,1},{2,3},{4,5},{6,7},{8,9},{10,11},{12,13},{14,15},{16,17},{18,... | collective-permute-start | bytes 147464 | tf_op jit(solution)/shard_map/ppermute | solution.py:28
  124.0 5.2 %collective-permute-start.22 = (f32[4,32,128]{2,1,0:T(8,128)}, f32[4,32,128]{2,1,0:T(8,128)S(1)}, u32[]{:S(2)}, u32[]{:S(2)}) collective-permute-start(f32[4,32,128]{2,1,0:T(8,128)} %get-tuple-element.111), channel_id=1, source_target_pairs={{0,2},{2,4},{4,6},{1,3},{3,5},{5,7},{8,10},{10,12},{12,14},{9,11},... | collective-permute-start | bytes 196616 | tf_op jit(solution)/shard_map/while/body/eval_jaxpr/ppermute | solution.py:28
  129.2 3.9 %collective-permute-start.4 = (f32[4,32,128]{2,1,0:T(8,128)S(1)}, f32[4,32,128]{2,1,0:T(8,128)S(1)}, u32[]{:S(2)}, u32[]{:S(2)}) collective-permute-start(f32[4,32,128]{2,1,0:T(8,128)S(1)} %get-tuple-element.107), channel_id=1, source_target_pairs={{0,2},{2,4},{4,6},{1,3},{3,5},{5,7},{8,10},{10,12},{12,14},{9,11},... | collective-permute-start | bytes 196616 | tf_op jit(solution)/shard_map/ppermute | solution.py:28
  137.4 4.7 %collective-permute-start.26 = (f32[24,4,128]{2,1,0:T(4,128)S(1)}, f32[24,4,128]{2,1,0:T(4,128)S(1)}, u32[]{:S(2)}, u32[]{:S(2)}) collective-permute-start(f32[24,4,128]{2,1,0:T(4,128)S(1)} %copy-done.21), channel_id=1, source_target_pairs={{0,1},{2,3},{4,5},{6,7},{8,9},{10,11},{12,13},{14,15},{16,17},{18,... | collective-permute-start | bytes 147464 | tf_op jit(solution)/shard_map/while/body/eval_jaxpr/ppermute | solution.py:28
  145.7 1.7 collective-permute-start.16
  149.6 4.8 %collective-permute-start.14 = (f32[8,32,128]{2,1,0:T(8,128)S(1)}, f32[8,32,128]{2,1,0:T(8,128)S(1)}, u32[]{:S(2)}, u32[]{:S(2)}) collective-permute-start(f32[8,32,128]{2,1,0:T(8,128)S(1)} %get-tuple-element.139), channel_id=1, source_target_pairs={{0,2},{2,4},{4,6},{1,3},{3,5},{5,7},{8,10},{10,12},{12,14},{9,11},... | collective-permute-start | bytes 393224 | tf_op jit(solution)/shard_map/while/body/eval_jaxpr/ppermute | solution.py:28
  156.9 4.8 %collective-permute-done.15 = f32[8,32,128]{2,1,0:T(8,128)S(1)} collective-permute-done((f32[8,32,128]{2,1,0:T(8,128)S(1)}, f32[8,32,128]{2,1,0:T(8,128)S(1)}, u32[]{:S(2)}, u32[]{:S(2)}) %collective-permute-start.15) | collective-permute-done | bytes 131104 | tf_op jit(solution)/shard_map/while/body/eval_jaxpr/ppermute | solution.py:31
  164.3 3.9 %collective-permute-start.20 = (f32[24,8,128]{2,1,0:T(8,128)S(1)}, f32[24,8,128]{2,1,0:T(8,128)S(1)}, u32[]{:S(2)}, u32[]{:S(2)}) collective-permute-start(f32[24,8,128]{2,1,0:T(8,128)S(1)} %get-tuple-element.137), channel_id=1, source_target_pairs={{0,1},{2,3},{4,5},{6,7},{8,9},{10,11},{12,13},{14,15},{16,17},{18,... | collective-permute-start | bytes 294920 | tf_op jit(solution)/shard_map/while/body/eval_jaxpr/ppermute | solution.py:28
  170.4 3.9 %collective-permute-start.18 = (f32[8,32,128]{2,1,0:T(8,128)S(1)}, f32[8,32,128]{2,1,0:T(8,128)S(1)}, u32[]{:S(2)}, u32[]{:S(2)}) collective-permute-start(f32[8,32,128]{2,1,0:T(8,128)S(1)} %get-tuple-element.135), channel_id=1, source_target_pairs={{0,2},{2,4},{4,6},{1,3},{3,5},{5,7},{8,10},{10,12},{12,14},{9,11},... | collective-permute-start | bytes 393224 | tf_op jit(solution)/shard_map/while/body/eval_jaxpr/ppermute | solution.py:28
  176.8 4.8 %collective-permute-done.19 = f32[8,32,128]{2,1,0:T(8,128)S(1)} collective-permute-done((f32[8,32,128]{2,1,0:T(8,128)S(1)}, f32[8,32,128]{2,1,0:T(8,128)S(1)}, u32[]{:S(2)}, u32[]{:S(2)}) %collective-permute-start.19) | collective-permute-done | bytes 131104 | tf_op jit(solution)/shard_map/while/body/eval_jaxpr/ppermute | solution.py:31
  184.6 1.8 fusion.190
  186.4 3.9 %collective-permute-start.28 = (f32[24,8,128]{2,1,0:T(8,128)S(1)}, f32[24,8,128]{2,1,0:T(8,128)S(1)}, u32[]{:S(2)}, u32[]{:S(2)}) collective-permute-start(f32[24,8,128]{2,1,0:T(8,128)S(1)} %get-tuple-element.133), channel_id=1, source_target_pairs={{0,1},{2,3},{4,5},{6,7},{8,9},{10,11},{12,13},{14,15},{16,17},{18,... | collective-permute-start | bytes 294920 | tf_op jit(solution)/shard_map/while/body/eval_jaxpr/ppermute | solution.py:28
  193.9 3.0 collective-permute-done.29
  196.9 2.8 collective-permute-start.24
  202.2 4.6 %collective-permute-done.25 = f32[8,32,128]{2,1,0:T(8,128)S(1)} collective-permute-done((f32[8,32,128]{2,1,0:T(8,128)S(1)}, f32[8,32,128]{2,1,0:T(8,128)S(1)}, u32[]{:S(2)}, u32[]{:S(2)}) %collective-permute-start.25) | collective-permute-done | bytes 131104 | tf_op jit(solution)/shard_map/while/body/eval_jaxpr/ppermute | solution.py:31
  212.5 1.9 collective-permute-start.30
  215.8 1.9 collective-permute-done.33
  218.3 3.1 collective-permute-done.31
  223.3 4.6 %collective-permute-start.36 = (f32[24,8,128]{2,1,0:T(8,128)S(1)}, f32[24,8,128]{2,1,0:T(8,128)S(1)}, u32[]{:S(2)}, u32[]{:S(2)}) collective-permute-start(f32[24,8,128]{2,1,0:T(8,128)S(1)} %get-tuple-element.123), channel_id=1, source_target_pairs={{0,1},{2,3},{4,5},{6,7},{8,9},{10,11},{12,13},{14,15},{16,17},{18,... | collective-permute-start | bytes 294920 | tf_op jit(solution)/shard_map/while/body/eval_jaxpr/ppermute | solution.py:28
  229.2 1.9 collective-permute-start.34
  232.6 1.7 collective-permute-done.37
  234.9 3.0 collective-permute-done.35
  241.0 2.1 copy.66
  243.2 2.1 reshape.234
  245.2 22.8 %reduce-scatter.4.cloned.1.call-done = f32[32,1536]{1,0:T(8,128)} async-done(((f32[128,1536]{1,0:T(8,128)}), f32[32,1536]{1,0:T(8,128)}) %reduce-scatter.4.cloned.1.call-update) | async-done | bytes 196624
  270.7 1.9 stack.27
  272.7 3.3 stack.28
  275.9 5.6 %maximum_bitcast_fusion = f32[8,6,8,2,4,4,4]{6,0,5,2,4,1,3:T(8,128)} fusion(f32[1,6,4,8,4,8,4]{6,5,4,3,2,1,0:T(8,128)} %stack.28, f32[1,6,4,8,4,8,4]{6,5,4,3,2,1,0:T(8,128)S(1)} %stack.27), kind=kLoop, calls=%fused_computation | loop fusion | flops 49152 | bytes 393216 | tf_op jit(solution)/shard_map/transpose | solution.py:130
  281.5 17.0 %copy.60 = f32[8,6,8,2,4,4,4]{2,1,0,6,5,4,3:T(8,128)} copy(f32[8,6,8,2,4,4,4]{6,0,5,2,4,1,3:T(8,128)} %maximum_bitcast_fusion) | data formatting | bytes 393216 | tf_op jit(solution)/shard_map/transpose | solution.py:130
  298.5 3.0 reshape.229
  302.9 40.3 %all-reduce.12 = (f32[64,64]{0,1:T(8,128)S(1)}, f32[64,128]{1,0:T(8,128)}) all-reduce(f32[64,64]{0,1:T(8,128)S(1)} %convolution_bitcast_fusion, f32[64,128]{1,0:T(8,128)S(1)} %fusion.408), channel_id=1, replica_groups=mesh['shot'=4,'gx'=4,'gy'=2] {'shot','gx','gy'}, use_global_device_ids=true, to_apply=%region_1.2 | all-reduce | flops 12288 | bytes 98304 | tf_op jit(solution)/shard_map/psum | solution.py:250
  (193 shorter events, 83.8 us)
Async XLA Ops:
  7.2 17.8 %copy-start = (f32[64,128]{1,0:T(8,128)S(1)}, f32[64,128]{1,0:T(8,128)}, u32[]{:S(2)}) copy-start(f32[64,128]{1,0:T(8,128)} %param.13) | copy-start | bytes 98308
  7.2 260.8 %reduce-scatter.4.cloned.1.call-start = ((), (), s32[]{:S(2)}) async-start(), calls=%async_computation.1 | async-start | bytes 983040
  8.9 83.2 %collective-permute-start.12 = (f32[24,8,128]{2,1,0:T(8,128)}, f32[24,8,128]{2,1,0:T(8,128)}, u32[]{:S(2)}, u32[]{:S(2)}) collective-permute-start(f32[24,8,128]{2,1,0:T(8,128)} %get-tuple-element.145), channel_id=1, source_target_pairs={{0,1},{2,3},{4,5},{6,7},{8,9},{10,11},{12,13},{14,15},{16,17},{18,... | collective-permute-start | bytes 294920 | tf_op jit(solution)/shard_map/while/body/eval_jaxpr/ppermute | solution.py:28
  14.3 82.9 %collective-permute-start.13 = (f32[24,8,128]{2,1,0:T(8,128)}, f32[24,8,128]{2,1,0:T(8,128)}, u32[]{:S(2)}, u32[]{:S(2)}) collective-permute-start(f32[24,8,128]{2,1,0:T(8,128)} %get-tuple-element.146), channel_id=1, source_target_pairs={{1,0},{3,2},{5,4},{7,6},{9,8},{11,10},{13,12},{15,14},{17,16},{19,... | collective-permute-start | bytes 294920 | tf_op jit(solution)/shard_map/while/body/eval_jaxpr/ppermute | solution.py:31
  17.3 86.7 %collective-permute-start.6 = (f32[8,32,128]{2,1,0:T(8,128)}, f32[8,32,128]{2,1,0:T(8,128)}, u32[]{:S(2)}, u32[]{:S(2)}) collective-permute-start(f32[8,32,128]{2,1,0:T(8,128)} %get-tuple-element.143), channel_id=1, source_target_pairs={{0,2},{2,4},{4,6},{1,3},{3,5},{5,7},{8,10},{10,12},{12,14},{9,11},... | collective-permute-start | bytes 393224 | tf_op jit(solution)/shard_map/while/body/eval_jaxpr/ppermute | solution.py:28
  21.5 83.8 %collective-permute-start.7 = (f32[8,32,128]{2,1,0:T(8,128)}, f32[8,32,128]{2,1,0:T(8,128)}, u32[]{:S(2)}, u32[]{:S(2)}) collective-permute-start(f32[8,32,128]{2,1,0:T(8,128)} %get-tuple-element.144), channel_id=1, source_target_pairs={{2,0},{4,2},{6,4},{3,1},{5,3},{7,5},{10,8},{12,10},{14,12},{11,9},... | collective-permute-start | bytes 393224 | tf_op jit(solution)/shard_map/while/body/eval_jaxpr/ppermute | solution.py:31
  50.4 39.5 %collective-permute-start = (f32[2,24,32,32]{3,2,1,0:T(8,128)S(1)}, f32[2,24,32,32]{3,2,1,0:T(8,128)S(1)}, u32[]{:S(2)}, u32[]{:S(2)}) collective-permute-start(f32[2,24,32,32]{3,2,1,0:T(8,128)S(1)} %pad_maximum_fusion), channel_id=1, source_target_pairs={{0,24},{8,0},{16,8},{24,16},{1,25},{9,1},{17,9},{25,17},{2,26},{10... | collective-permute-start | bytes 589832 | tf_op jit(solution)/shard_map/ppermute | solution.py:16
  54.7 17.9 %copy-start.7 = (f32[24,32,128]{2,1,0:T(8,128)}, f32[24,32,128]{2,1,0:T(8,128)S(1)}, u32[]{:S(2)}) copy-start(f32[24,32,128]{2,1,0:T(8,128)S(1)} %get-tuple-element.118) | copy-start | bytes 1179652
  58.3 30.9 %copy-start.8 = (f32[24,32,128]{2,1,0:T(8,128)}, f32[24,32,128]{2,1,0:T(8,128)S(1)}, u32[]{:S(2)}) copy-start(f32[24,32,128]{2,1,0:T(8,128)S(1)} %get-tuple-element.114) | copy-start | bytes 1179652
  76.7 26.3 %copy-start.1 = (f32[1,24,32,128]{3,2,1,0:T(8,128)S(1)}, f32[1,24,32,128]{3,2,1,0:T(8,128)}, u32[]{:S(2)}) copy-start(f32[1,24,32,128]{3,2,1,0:T(8,128)} %param.14) | copy-start | bytes 1179652
  90.2 19.7 %collective-permute-start.1 = (f32[2,24,32,64]{3,2,1,0:T(8,128)S(1)}, f32[2,24,32,64]{3,2,1,0:T(8,128)}, u32[]{:S(2)}, u32[]{:S(2)}) collective-permute-start(f32[2,24,32,64]{3,2,1,0:T(8,128)S(1)} %pad_maximum_fusion.1), channel_id=1, source_target_pairs={{0,16},{8,24},{16,0},{24,8},{1,17},{9,25},{17,1},{25,9},{2,18},{10... | collective-permute-start | bytes 1179656 | tf_op jit(solution)/shard_map/ppermute | solution.py:16
  92.0 44.0 %collective-permute-start.2 = (f32[4,32,128]{2,1,0:T(8,128)}, f32[4,32,128]{2,1,0:T(8,128)}, u32[]{:S(2)}, u32[]{:S(2)}) collective-permute-start(f32[4,32,128]{2,1,0:T(8,128)} %get-tuple-element.115), channel_id=1, source_target_pairs={{0,2},{2,4},{4,6},{1,3},{3,5},{5,7},{8,10},{10,12},{12,14},{9,11},... | collective-permute-start | bytes 196616 | tf_op jit(solution)/shard_map/while/body/eval_jaxpr/ppermute | solution.py:28
  97.2 25.4 %collective-permute-start.8 = (f32[24,4,128]{2,1,0:T(4,128)}, f32[24,4,128]{2,1,0:T(4,128)}, u32[]{:S(2)}, u32[]{:S(2)}) collective-permute-start(f32[24,4,128]{2,1,0:T(4,128)} %get-tuple-element.151), channel_id=1, source_target_pairs={{0,1},{2,3},{4,5},{6,7},{8,9},{10,11},{12,13},{14,15},{16,17},{18,... | collective-permute-start | bytes 147464 | tf_op jit(solution)/shard_map/while/body/eval_jaxpr/ppermute | solution.py:28
  104.0 20.0 %collective-permute-start.9 = (f32[24,4,128]{2,1,0:T(4,128)}, f32[24,4,128]{2,1,0:T(4,128)}, u32[]{:S(2)}, u32[]{:S(2)}) collective-permute-start(f32[24,4,128]{2,1,0:T(4,128)} %get-tuple-element.152), channel_id=1, source_target_pairs={{1,0},{3,2},{5,4},{7,6},{9,8},{11,10},{13,12},{15,14},{17,16},{19,... | collective-permute-start | bytes 147464 | tf_op jit(solution)/shard_map/while/body/eval_jaxpr/ppermute | solution.py:31
  115.9 20.2 %copy-start.19 = (f32[4,32,128]{2,1,0:T(8,128)S(1)}, f32[4,32,128]{2,1,0:T(8,128)}, u32[]{:S(2)}) copy-start(f32[4,32,128]{2,1,0:T(8,128)} %get-tuple-element.112) | copy-start | bytes 196612
  115.9 21.5 %copy-start.21 = (f32[24,4,128]{2,1,0:T(4,128)S(1)}, f32[24,4,128]{2,1,0:T(4,128)}, u32[]{:S(2)}) copy-start(f32[24,4,128]{2,1,0:T(4,128)} %get-tuple-element.131) | copy-start | bytes 147460
  115.9 26.2 %copy-start.16 = (f32[24,32,128]{2,1,0:T(8,128)S(1)}, f32[24,32,128]{2,1,0:T(8,128)}, u32[]{:S(2)}) copy-start(f32[24,32,128]{2,1,0:T(8,128)} %get-tuple-element.117) | copy-start | bytes 1179652
  115.9 13.2 %collective-permute-start.10 = (f32[24,4,128]{2,1,0:T(4,128)S(1)}, f32[24,4,128]{2,1,0:T(4,128)S(1)}, u32[]{:S(2)}, u32[]{:S(2)}) collective-permute-start(f32[24,4,128]{2,1,0:T(4,128)S(1)} %get-tuple-element.147), channel_id=1, source_target_pairs={{0,1},{2,3},{4,5},{6,7},{8,9},{10,11},{12,13},{14,15},{16,17},{18,... | collective-permute-start | bytes 147464 | tf_op jit(solution)/shard_map/ppermute | solution.py:28
  121.2 11.9 %collective-permute-start.11 = (f32[24,4,128]{2,1,0:T(4,128)S(1)}, f32[24,4,128]{2,1,0:T(4,128)S(1)}, u32[]{:S(2)}, u32[]{:S(2)}) collective-permute-start(f32[24,4,128]{2,1,0:T(4,128)S(1)} %get-tuple-element.148), channel_id=1, source_target_pairs={{1,0},{3,2},{5,4},{7,6},{9,8},{11,10},{13,12},{15,14},{17,16},{19,... | collective-permute-start | bytes 147464 | tf_op jit(solution)/shard_map/ppermute | solution.py:31
  122.7 14.7 %collective-permute-start.3 = (f32[4,32,128]{2,1,0:T(8,128)}, f32[4,32,128]{2,1,0:T(8,128)S(1)}, u32[]{:S(2)}, u32[]{:S(2)}) collective-permute-start(f32[4,32,128]{2,1,0:T(8,128)} %get-tuple-element.116), channel_id=1, source_target_pairs={{2,0},{4,2},{6,4},{3,1},{5,3},{7,5},{10,8},{12,10},{14,12},{11,9},... | collective-permute-start | bytes 196616 | tf_op jit(solution)/shard_map/while/body/eval_jaxpr/ppermute | solution.py:31
  124.0 82.9 %collective-permute-start.22 = (f32[4,32,128]{2,1,0:T(8,128)}, f32[4,32,128]{2,1,0:T(8,128)S(1)}, u32[]{:S(2)}, u32[]{:S(2)}) collective-permute-start(f32[4,32,128]{2,1,0:T(8,128)} %get-tuple-element.111), channel_id=1, source_target_pairs={{0,2},{2,4},{4,6},{1,3},{3,5},{5,7},{8,10},{10,12},{12,14},{9,11},... | collective-permute-start | bytes 196616 | tf_op jit(solution)/shard_map/while/body/eval_jaxpr/ppermute | solution.py:28
  129.2 12.9 %collective-permute-start.4 = (f32[4,32,128]{2,1,0:T(8,128)S(1)}, f32[4,32,128]{2,1,0:T(8,128)S(1)}, u32[]{:S(2)}, u32[]{:S(2)}) collective-permute-start(f32[4,32,128]{2,1,0:T(8,128)S(1)} %get-tuple-element.107), channel_id=1, source_target_pairs={{0,2},{2,4},{4,6},{1,3},{3,5},{5,7},{8,10},{10,12},{12,14},{9,11},... | collective-permute-start | bytes 196616 | tf_op jit(solution)/shard_map/ppermute | solution.py:28
  133.1 9.0 %collective-permute-start.5 = (f32[4,32,128]{2,1,0:T(8,128)S(1)}, f32[4,32,128]{2,1,0:T(8,128)S(1)}, u32[]{:S(2)}, u32[]{:S(2)}) collective-permute-start(f32[4,32,128]{2,1,0:T(8,128)S(1)} %get-tuple-element.108), channel_id=1, source_target_pairs={{2,0},{4,2},{6,4},{3,1},{5,3},{7,5},{10,8},{12,10},{14,12},{11,9},... | collective-permute-start | bytes 196616 | tf_op jit(solution)/shard_map/ppermute | solution.py:31
  136.0 70.8 %collective-permute-start.23 = (f32[4,32,128]{2,1,0:T(8,128)S(1)}, f32[4,32,128]{2,1,0:T(8,128)S(1)}, u32[]{:S(2)}, u32[]{:S(2)}) collective-permute-start(f32[4,32,128]{2,1,0:T(8,128)S(1)} %copy-done.19), channel_id=1, source_target_pairs={{2,0},{4,2},{6,4},{3,1},{5,3},{7,5},{10,8},{12,10},{14,12},{11,9},... | collective-permute-start | bytes 196616 | tf_op jit(solution)/shard_map/while/body/eval_jaxpr/ppermute | solution.py:31
  137.4 62.4 %collective-permute-start.26 = (f32[24,4,128]{2,1,0:T(4,128)S(1)}, f32[24,4,128]{2,1,0:T(4,128)S(1)}, u32[]{:S(2)}, u32[]{:S(2)}) collective-permute-start(f32[24,4,128]{2,1,0:T(4,128)S(1)} %copy-done.21), channel_id=1, source_target_pairs={{0,1},{2,3},{4,5},{6,7},{8,9},{10,11},{12,13},{14,15},{16,17},{18,... | collective-permute-start | bytes 147464 | tf_op jit(solution)/shard_map/while/body/eval_jaxpr/ppermute | solution.py:28
  145.7 3.9 %collective-permute-start.16 = (f32[24,8,128]{2,1,0:T(8,128)S(1)}, f32[24,8,128]{2,1,0:T(8,128)S(1)}, u32[]{:S(2)}, u32[]{:S(2)}) collective-permute-start(f32[24,8,128]{2,1,0:T(8,128)S(1)} %get-tuple-element.141), channel_id=1, source_target_pairs={{0,1},{2,3},{4,5},{6,7},{8,9},{10,11},{12,13},{14,15},{16,17},{18,... | collective-permute-start | bytes 294920 | tf_op jit(solution)/shard_map/while/body/eval_jaxpr/ppermute | solution.py:28
  147.4 7.0 %collective-permute-start.17 = (f32[24,8,128]{2,1,0:T(8,128)S(1)}, f32[24,8,128]{2,1,0:T(8,128)S(1)}, u32[]{:S(2)}, u32[]{:S(2)}) collective-permute-start(f32[24,8,128]{2,1,0:T(8,128)S(1)} %get-tuple-element.142), channel_id=1, source_target_pairs={{1,0},{3,2},{5,4},{7,6},{9,8},{11,10},{13,12},{15,14},{17,16},{19,... | collective-permute-start | bytes 294920 | tf_op jit(solution)/shard_map/while/body/eval_jaxpr/ppermute | solution.py:31
  149.6 7.3 %collective-permute-start.14 = (f32[8,32,128]{2,1,0:T(8,128)S(1)}, f32[8,32,128]{2,1,0:T(8,128)S(1)}, u32[]{:S(2)}, u32[]{:S(2)}) collective-permute-start(f32[8,32,128]{2,1,0:T(8,128)S(1)} %get-tuple-element.139), channel_id=1, source_target_pairs={{0,2},{2,4},{4,6},{1,3},{3,5},{5,7},{8,10},{10,12},{12,14},{9,11},... | collective-permute-start | bytes 393224 | tf_op jit(solution)/shard_map/while/body/eval_jaxpr/ppermute | solution.py:28
  154.4 7.2 %collective-permute-start.15 = (f32[8,32,128]{2,1,0:T(8,128)S(1)}, f32[8,32,128]{2,1,0:T(8,128)S(1)}, u32[]{:S(2)}, u32[]{:S(2)}) collective-permute-start(f32[8,32,128]{2,1,0:T(8,128)S(1)} %get-tuple-element.140), channel_id=1, source_target_pairs={{2,0},{4,2},{6,4},{3,1},{5,3},{7,5},{10,8},{12,10},{14,12},{11,9},... | collective-permute-start | bytes 393224 | tf_op jit(solution)/shard_map/while/body/eval_jaxpr/ppermute | solution.py:31
  164.3 6.1 %collective-permute-start.20 = (f32[24,8,128]{2,1,0:T(8,128)S(1)}, f32[24,8,128]{2,1,0:T(8,128)S(1)}, u32[]{:S(2)}, u32[]{:S(2)}) collective-permute-start(f32[24,8,128]{2,1,0:T(8,128)S(1)} %get-tuple-element.137), channel_id=1, source_target_pairs={{0,1},{2,3},{4,5},{6,7},{8,9},{10,11},{12,13},{14,15},{16,17},{18,... | collective-permute-start | bytes 294920 | tf_op jit(solution)/shard_map/while/body/eval_jaxpr/ppermute | solution.py:28
  168.2 6.5 %collective-permute-start.21 = (f32[24,8,128]{2,1,0:T(8,128)S(1)}, f32[24,8,128]{2,1,0:T(8,128)S(1)}, u32[]{:S(2)}, u32[]{:S(2)}) collective-permute-start(f32[24,8,128]{2,1,0:T(8,128)S(1)} %get-tuple-element.138), channel_id=1, source_target_pairs={{1,0},{3,2},{5,4},{7,6},{9,8},{11,10},{13,12},{15,14},{17,16},{19,... | collective-permute-start | bytes 294920 | tf_op jit(solution)/shard_map/while/body/eval_jaxpr/ppermute | solution.py:31
  170.4 6.4 %collective-permute-start.18 = (f32[8,32,128]{2,1,0:T(8,128)S(1)}, f32[8,32,128]{2,1,0:T(8,128)S(1)}, u32[]{:S(2)}, u32[]{:S(2)}) collective-permute-start(f32[8,32,128]{2,1,0:T(8,128)S(1)} %get-tuple-element.135), channel_id=1, source_target_pairs={{0,2},{2,4},{4,6},{1,3},{3,5},{5,7},{8,10},{10,12},{12,14},{9,11},... | collective-permute-start | bytes 393224 | tf_op jit(solution)/shard_map/while/body/eval_jaxpr/ppermute | solution.py:28
  174.7 6.8 %collective-permute-start.19 = (f32[8,32,128]{2,1,0:T(8,128)S(1)}, f32[8,32,128]{2,1,0:T(8,128)S(1)}, u32[]{:S(2)}, u32[]{:S(2)}) collective-permute-start(f32[8,32,128]{2,1,0:T(8,128)S(1)} %get-tuple-element.136), channel_id=1, source_target_pairs={{2,0},{4,2},{6,4},{3,1},{5,3},{7,5},{10,8},{12,10},{14,12},{11,9},... | collective-permute-start | bytes 393224 | tf_op jit(solution)/shard_map/while/body/eval_jaxpr/ppermute | solution.py:31
  186.4 6.1 %collective-permute-start.28 = (f32[24,8,128]{2,1,0:T(8,128)S(1)}, f32[24,8,128]{2,1,0:T(8,128)S(1)}, u32[]{:S(2)}, u32[]{:S(2)}) collective-permute-start(f32[24,8,128]{2,1,0:T(8,128)S(1)} %get-tuple-element.133), channel_id=1, source_target_pairs={{0,1},{2,3},{4,5},{6,7},{8,9},{10,11},{12,13},{14,15},{16,17},{18,... | collective-permute-start | bytes 294920 | tf_op jit(solution)/shard_map/while/body/eval_jaxpr/ppermute | solution.py:28
  190.4 6.5 %collective-permute-start.29 = (f32[24,8,128]{2,1,0:T(8,128)S(1)}, f32[24,8,128]{2,1,0:T(8,128)S(1)}, u32[]{:S(2)}, u32[]{:S(2)}) collective-permute-start(f32[24,8,128]{2,1,0:T(8,128)S(1)} %get-tuple-element.134), channel_id=1, source_target_pairs={{1,0},{3,2},{5,4},{7,6},{9,8},{11,10},{13,12},{15,14},{17,16},{19,... | collective-permute-start | bytes 294920 | tf_op jit(solution)/shard_map/while/body/eval_jaxpr/ppermute | solution.py:31
  192.6 8.7 %collective-permute-start.27 = (f32[24,4,128]{2,1,0:T(4,128)S(1)}, f32[24,4,128]{2,1,0:T(4,128)S(1)}, u32[]{:S(2)}, u32[]{:S(2)}) collective-permute-start(f32[24,4,128]{2,1,0:T(4,128)S(1)} %copy-done.20), channel_id=1, source_target_pairs={{1,0},{3,2},{5,4},{7,6},{9,8},{11,10},{13,12},{15,14},{17,16},{19,... | collective-permute-start | bytes 147464 | tf_op jit(solution)/shard_map/while/body/eval_jaxpr/ppermute | solution.py:31
  196.9 5.3 %collective-permute-start.24 = (f32[8,32,128]{2,1,0:T(8,128)S(1)}, f32[8,32,128]{2,1,0:T(8,128)S(1)}, u32[]{:S(2)}, u32[]{:S(2)}) collective-permute-start(f32[8,32,128]{2,1,0:T(8,128)S(1)} %get-tuple-element.129), channel_id=1, source_target_pairs={{0,2},{2,4},{4,6},{1,3},{3,5},{5,7},{8,10},{10,12},{12,14},{9,11},... | collective-permute-start | bytes 393224 | tf_op jit(solution)/shard_map/while/body/eval_jaxpr/ppermute | solution.py:28
  199.8 7.0 %collective-permute-start.25 = (f32[8,32,128]{2,1,0:T(8,128)S(1)}, f32[8,32,128]{2,1,0:T(8,128)S(1)}, u32[]{:S(2)}, u32[]{:S(2)}) collective-permute-start(f32[8,32,128]{2,1,0:T(8,128)S(1)} %get-tuple-element.130), channel_id=1, source_target_pairs={{2,0},{4,2},{6,4},{3,1},{5,3},{7,5},{10,8},{12,10},{14,12},{11,9},... | collective-permute-start | bytes 393224 | tf_op jit(solution)/shard_map/while/body/eval_jaxpr/ppermute | solution.py:31
  209.7 6.1 %collective-permute-start.32 = (f32[24,8,128]{2,1,0:T(8,128)S(1)}, f32[24,8,128]{2,1,0:T(8,128)S(1)}, u32[]{:S(2)}, u32[]{:S(2)}) collective-permute-start(f32[24,8,128]{2,1,0:T(8,128)S(1)} %get-tuple-element.127), channel_id=1, source_target_pairs={{0,1},{2,3},{4,5},{6,7},{8,9},{10,11},{12,13},{14,15},{16,17},{18,... | collective-permute-start | bytes 294920 | tf_op jit(solution)/shard_map/while/body/eval_jaxpr/ppermute | solution.py:28
  211.2 6.5 %collective-permute-start.33 = (f32[24,8,128]{2,1,0:T(8,128)S(1)}, f32[24,8,128]{2,1,0:T(8,128)S(1)}, u32[]{:S(2)}, u32[]{:S(2)}) collective-permute-start(f32[24,8,128]{2,1,0:T(8,128)S(1)} %get-tuple-element.128), channel_id=1, source_target_pairs={{1,0},{3,2},{5,4},{7,6},{9,8},{11,10},{13,12},{15,14},{17,16},{19,... | collective-permute-start | bytes 294920 | tf_op jit(solution)/shard_map/while/body/eval_jaxpr/ppermute | solution.py:31
  212.5 5.7 %collective-permute-start.30 = (f32[8,32,128]{2,1,0:T(8,128)S(1)}, f32[8,32,128]{2,1,0:T(8,128)S(1)}, u32[]{:S(2)}, u32[]{:S(2)}) collective-permute-start(f32[8,32,128]{2,1,0:T(8,128)S(1)} %get-tuple-element.125), channel_id=1, source_target_pairs={{0,2},{2,4},{4,6},{1,3},{3,5},{5,7},{8,10},{10,12},{12,14},{9,11},... | collective-permute-start | bytes 393224 | tf_op jit(solution)/shard_map/while/body/eval_jaxpr/ppermute | solution.py:28
  214.5 6.9 %collective-permute-start.31 = (f32[8,32,128]{2,1,0:T(8,128)S(1)}, f32[8,32,128]{2,1,0:T(8,128)S(1)}, u32[]{:S(2)}, u32[]{:S(2)}) collective-permute-start(f32[8,32,128]{2,1,0:T(8,128)S(1)} %get-tuple-element.126), channel_id=1, source_target_pairs={{2,0},{4,2},{6,4},{3,1},{5,3},{7,5},{10,8},{12,10},{14,12},{11,9},... | collective-permute-start | bytes 393224 | tf_op jit(solution)/shard_map/while/body/eval_jaxpr/ppermute | solution.py:31
  223.3 9.3 %collective-permute-start.36 = (f32[24,8,128]{2,1,0:T(8,128)S(1)}, f32[24,8,128]{2,1,0:T(8,128)S(1)}, u32[]{:S(2)}, u32[]{:S(2)}) collective-permute-start(f32[24,8,128]{2,1,0:T(8,128)S(1)} %get-tuple-element.123), channel_id=1, source_target_pairs={{0,1},{2,3},{4,5},{6,7},{8,9},{10,11},{12,13},{14,15},{16,17},{18,... | collective-permute-start | bytes 294920 | tf_op jit(solution)/shard_map/while/body/eval_jaxpr/ppermute | solution.py:28
  227.8 6.5 %collective-permute-start.37 = (f32[24,8,128]{2,1,0:T(8,128)S(1)}, f32[24,8,128]{2,1,0:T(8,128)S(1)}, u32[]{:S(2)}, u32[]{:S(2)}) collective-permute-start(f32[24,8,128]{2,1,0:T(8,128)S(1)} %get-tuple-element.124), channel_id=1, source_target_pairs={{1,0},{3,2},{5,4},{7,6},{9,8},{11,10},{13,12},{15,14},{17,16},{19,... | collective-permute-start | bytes 294920 | tf_op jit(solution)/shard_map/while/body/eval_jaxpr/ppermute | solution.py:31
  229.2 5.7 %collective-permute-start.34 = (f32[8,32,128]{2,1,0:T(8,128)S(1)}, f32[8,32,128]{2,1,0:T(8,128)S(1)}, u32[]{:S(2)}, u32[]{:S(2)}) collective-permute-start(f32[8,32,128]{2,1,0:T(8,128)S(1)} %get-tuple-element.121), channel_id=1, source_target_pairs={{0,2},{2,4},{4,6},{1,3},{3,5},{5,7},{8,10},{10,12},{12,14},{9,11},... | collective-permute-start | bytes 393224 | tf_op jit(solution)/shard_map/while/body/eval_jaxpr/ppermute | solution.py:28
  231.1 6.9 %collective-permute-start.35 = (f32[8,32,128]{2,1,0:T(8,128)S(1)}, f32[8,32,128]{2,1,0:T(8,128)S(1)}, u32[]{:S(2)}, u32[]{:S(2)}) collective-permute-start(f32[8,32,128]{2,1,0:T(8,128)S(1)} %get-tuple-element.122), channel_id=1, source_target_pairs={{2,0},{4,2},{6,4},{3,1},{5,3},{7,5},{10,8},{12,10},{14,12},{11,9},... | collective-permute-start | bytes 393224 | tf_op jit(solution)/shard_map/while/body/eval_jaxpr/ppermute | solution.py:31
  245.2 24.4 %copy-start.5 = (f32[1,24,32,32]{3,2,1,0:T(8,128)S(1)}, f32[1,24,32,32]{3,2,1,0:T(8,128)}, u32[]{:S(2)}) copy-start(f32[1,24,32,32]{3,2,1,0:T(8,128)} %div.74) | copy-start | bytes 294916
  245.2 24.4 %copy-start.6 = (f32[1,24,32,32]{3,2,1,0:T(8,128)S(1)}, f32[1,24,32,32]{3,2,1,0:T(8,128)}, u32[]{:S(2)}) copy-start(f32[1,24,32,32]{3,2,1,0:T(8,128)} %div.72) | copy-start | bytes 294916
  (17 other events, 119.8 us)
Sparse Core Ops, SparseCore 0:
  245.4 22.6 reduce-scatter.3
